TPU v7x, 256 devices: a whole 4x4x8 slice. The times are simulated.
256 devices in a mesh: grp: 8 (over z_hi, x), dev: 32 (over y, z_lo, core).
Axes of the slice: x: 4, y: 4, z: 8 (z_hi: 2, z_lo: 4; z = z_hi * 4 + z_lo), core: 2. Of those that a mesh axis runs over, the one named last changes fastest.
Arguments:
- step_number: int32 [], replicated, may hold values from 0 to 999
- power_maps: bfloat16 [2048, 64, 128], P(('grp', 'dev')), may hold values from -6 to 6
- heat_maps: bfloat16 [2048, 1024], P(('grp', 'dev')), may hold values from -6 to 6
- home_table: int32 [8, 256], P('grp'), may hold values from 0 to 255, as said below
- requests: int32 [256, 32], P(('grp', 'dev')), may hold values from 0 to 255, as said below
- counts: int32 [256], P(('grp', 'dev')), may hold values from 1 to 32, as said below
- stem_weight: float32 [256, 128, 256], P(('grp', 'dev')), may hold values from -0.5 to 0.5
- conv_weight: float32 [256, 2, 2304, 256], P(('grp', 'dev')), may hold values from -0.125 to 0.125
- head_weight: float32 [256, 16, 256], P(('grp', 'dev')), may hold values from -0.375 to 0.375
- biases: float32 [256, 3, 256], P(('grp', 'dev')), may hold values from -3 to 3
Outputs:
- new_stem: float32 [256, 128, 256], P(('grp', 'dev'))
- new_conv: float32 [256, 2, 2304, 256], P(('grp', 'dev'))
- new_head: float32 [256, 16, 256], P(('grp', 'dev'))
- new_biases: float32 [256, 3, 256], P(('grp', 'dev'))
- grad_stem: bfloat16 [256, 128, 256], P(('grp', 'dev'))
- grad_conv: bfloat16 [256, 2, 2304, 256], P(('grp', 'dev'))
- grad_head: bfloat16 [256, 16, 256], P(('grp', 'dev'))
- grad_biases: bfloat16 [256, 3, 256], P(('grp', 'dev'))
Inputs may be any that keep to these rules, and one draw needn't show every extreme that they name: Each row is a permutation; sample s of group g is stored by dev index home_table[g, s] // 8 as its local sample home_table[g, s] % 8. Among the live requests of one device (its first counts entries) at most 2 are stored by any one dev index; in every group some device has exactly 2 from one dev index. `counts`: in every group some device has 32 live requests.
All inputs are finite; a program needn't handle non-finite values.
Results may differ from a plain program's by a relative error of at most 0.024.
The roundings to bfloat16 on the way count: a program that leaves them out, or rounds other values in their place, can miss the bound.
Values may be sent and summed in bfloat16 or wider, within the bound.
No kernel may reach another device: no remote copies, remote signals or barrier semaphores. Data moves between devices by JAX's collectives and lax.ppermute only.
A program may use at most 128 MiB of HBM per device.

v0:
```python
import functools

import jax
import jax.numpy as jnp
from jax import lax
from jax.experimental import pallas as pl
from jax.experimental.pallas import tpu as pltpu
from jax.sharding import PartitionSpec as P

bf16 = jnp.bfloat16
f32 = jnp.float32
NT = (((1,), (1,)), ((), ()))
TN = (((0,), (0,)), ((), ()))
ROW_STEM = 4608
ROW_HEAD = 4736
PACKED = 4768


def dot(a, b):
    return jnp.dot(a, b, preferred_element_type=f32)


def block(i, n):
    return pl.ds(pl.multiple_of(i * n, n), n)


def main_kernel(
    count_ref, scale_ref, slot_ref, sel_ref, got_ref, w_hbm, bias_ref, conv_hbm, stem_ref, head_ref,
    gconv_hbm, base_hbm, gstem_ref, ghead_ref, gbias_ref, bstem_ref, bhead_ref, bbias_ref,
    wb, mine, gb, x_s, heat_s, act, act_t, grad, whe, err_s, err_t, bsum, gstem_acc,
    wsem, msem, osem, gsem, *, U, UB):
    wcopies = []
    for k, (lo, n) in enumerate(((ROW_STEM, PACKED - ROW_STEM), (0, ROW_STEM))):
        c = pltpu.make_async_copy(w_hbm.at[slot_ref[0], pl.ds(lo, n)], wb.at[pl.ds(lo, n)], wsem.at[k])
        c.start()
        wcopies.append(c)
    load_mine = pltpu.make_async_copy(conv_hbm, mine, msem)
    load_mine.start()

    edge = jnp.zeros((32, 256), bf16)

    @pl.loop(0, 10)
    def _(q):
        for buf, ks in ((act, (0, 1)), (grad, (1, 2))):
            for k in ks:
                buf[k, 0, block(q, 32), :] = edge
                buf[k, 9, block(q, 32), :] = edge
                buf[k, q, 0:32, :] = edge
                buf[k, q, 288:320, :] = edge

    sel = sel_ref[...]
    wcopies[0].wait()
    ws = wb[ROW_STEM:ROW_STEM + 128, :]
    b0 = bias_ref[0:1, :]

    @pl.loop(0, 8)
    def _(u):
        r = dot(sel, got_ref[:, block(u, 1024)]).astype(bf16)
        x = jnp.concatenate([r[:, v * 128:(v + 1) * 128] for v in range(8)], axis=0)
        x_s[u] = x
        heat_s[block(u, 32), :] = dot(sel, got_ref[:, pl.ds(pl.multiple_of(8192 + u * 128, 128), 128)])
        pre = dot(x, ws) + b0
        a = jnp.maximum(pre, 0.0).astype(bf16)
        act[0, u + 1, 32:288, :] = a
        act_t[0, :, block(u, 256)] = a.T

    wcopies[1].wait()
    n = 8 // U

    @pl.loop(0, 2 * n)
    def _(k):
        s = k // n
        u = (k - s * n) * U
        rows = []
        for e in range(U):
            rows.append(jnp.concatenate(
                [act[s, u + e + i, j * 32:j * 32 + 256, :] for i in range(3) for j in range(3)], axis=1))
        lhs = rows[0] if U == 1 else jnp.concatenate(rows, axis=0)
        pre = dot(lhs, wb[block(s, 2304), :]) + bias_ref[pl.ds(s + 1, 1), :]
        keep = s.astype(f32)
        for e in range(U):
            p = pre[e * 256:(e + 1) * 256] + keep * act[0, u + e + 1, 32:288, :].astype(f32)
            a = jnp.maximum(p, 0.0).astype(bf16)
            act[s + 1, u + e + 1, 32:288, :] = a
            act_t[s + 1, :, block(u + e, 256)] = a.T

    count = count_ref[0]
    scale = scale_ref[0]
    wh = wb[ROW_HEAD:ROW_HEAD + 16, :]

    def predict(v, pred):
        whe[v] = jnp.zeros((128, 256), bf16)
        whe[v, block(v, 16), :] = wh
        a = act[2, 1:9, pl.ds(pl.multiple_of(v * 32 + 32, 32), 32), :].reshape(256, 256)
        return pred + lax.dot_general(a, whe[v], NT, preferred_element_type=f32)

    pred = lax.fori_loop(0, 8, predict, jnp.zeros((256, 128), f32))
    row = lax.broadcasted_iota(jnp.int32, (256, 128), 0)
    err = jnp.where((row & 31) < count, (pred - heat_s[...]) * scale, 0.0).astype(bf16)
    err_s[...] = err
    err_t[...] = err.T
    bsum[...] = jnp.zeros_like(bsum)

    def spread(v, gh):
        at = pl.ds(pl.multiple_of(v * 32 + 32, 32), 32)
        a = act[2, 1:9, at, :].reshape(256, 256)
        d = jnp.where(a > 0, dot(err_s[...], whe[v]), 0.0).astype(bf16)
        bsum[2:3, :] += jnp.sum(d.astype(f32), axis=0, keepdims=True)
        grad[2, 1:9, at, :] = d.reshape(8, 32, 256)
        return gh + dot(err_t[block(v, 16), :], a)

    gh = lax.fori_loop(0, 8, spread, jnp.zeros((16, 256), f32))
    ghead_ref[...] = gh.astype(bf16)
    bhead_ref[...] = 0.5 * head_ref[...] - 0.1 * gh

    m = 8 // UB

    @pl.loop(0, 2 * m)
    def _(k):
        q = k // m
        s = 1 - q
        u = (k - q * m) * UB
        da = None
        for i in range(3):
            for j in range(3):
                ii, jj = 2 - i, 2 - j
                rows = [grad[s + 1, u + e + ii, jj * 32:jj * 32 + 256, :] for e in range(UB)]
                lhs = rows[0] if UB == 1 else jnp.concatenate(rows, axis=0)
                w = wb[pl.ds(pl.multiple_of(s * 2304 + (3 * i + j) * 256, 256), 256), :]
                t = lax.dot_general(lhs, w, NT, preferred_element_type=f32)
                da = t if da is None else da + t
        keep = q.astype(f32)
        for e in range(UB):
            d = da[e * 256:(e + 1) * 256] + keep * grad[2, u + e + 1, 32:288, :].astype(f32)
            d = jnp.where(act[s, u + e + 1, 32:288, :] > 0, d, 0.0).astype(bf16)
            grad[s, u + e + 1, 32:288, :] = d
            bsum[pl.ds(s, 1), :] += jnp.sum(d.astype(f32), axis=0, keepdims=True)

    gbias_ref[...] = bsum[0:3, :].astype(bf16)
    bbias_ref[...] = 0.5 * bias_ref[...] - 0.1 * bsum[0:3, :]
    gstem_acc[...] = jnp.zeros_like(gstem_acc)

    @pl.loop(0, 8)
    def _(u):
        gstem_acc[...] += lax.dot_general(x_s[u], grad[0, u + 1, 32:288, :], TN, preferred_element_type=f32)

    gs = gstem_acc[...]
    gstem_ref[...] = gs.astype(bf16)
    bstem_ref[...] = 0.5 * stem_ref[...] - 0.1 * gs

    load_mine.wait()

    def outs(t):
        r = block(t, 256)
        return (pltpu.make_async_copy(gb.at[r], gconv_hbm.at[r], gsem.at[t]),
                pltpu.make_async_copy(mine.at[r], base_hbm.at[r], osem.at[t]))

    @pl.loop(0, 18)
    def _(t):
        s = t // 9
        tap = t - s * 9
        ii = 2 - tap // 3
        jj = 2 - tap % 3
        rhs = jnp.concatenate([grad[s + 1, u + ii, pl.ds(pl.multiple_of(jj * 32, 32), 256), :] for u in range(8)], axis=0)
        g = dot(act_t[s], rhs)
        r = block(t, 256)
        gb[r, :] = g.astype(bf16)
        mine[r, :] = 0.5 * mine[r, :] - 0.1 * g
        for c in outs(t):
            c.start()

    @pl.loop(0, 18)
    def _(t):
        for c in outs(t):
            c.wait()


def main_call(count, scale, slot, sel, got, packed, bias, conv, stem, head, U=2, UB=2):
    vm = pl.BlockSpec(memory_space=pltpu.VMEM)
    sm = pl.BlockSpec(memory_space=pltpu.SMEM)
    hb = pl.BlockSpec(memory_space=pltpu.HBM)
    S = jax.ShapeDtypeStruct
    maps = pltpu.VMEM((3, 10, 320, 256), bf16)
    return pl.pallas_call(
        functools.partial(main_kernel, U=U, UB=UB),
        out_shape=(S((4608, 256), bf16), S((4608, 256), f32), S((128, 256), bf16), S((16, 256), bf16), S((3, 256), bf16),
                   S((128, 256), f32), S((16, 256), f32), S((3, 256), f32)),
        in_specs=[sm, sm, sm, vm, vm, hb, vm, hb, vm, vm],
        out_specs=(hb, hb, vm, vm, vm, vm, vm, vm),
        scratch_shapes=[
            pltpu.VMEM((PACKED, 256), bf16), pltpu.VMEM((4608, 256), f32), pltpu.VMEM((4608, 256), bf16),
            pltpu.VMEM((8, 256, 128), bf16), pltpu.VMEM((256, 128), f32), maps, pltpu.VMEM((3, 256, 2048), bf16), maps,
            pltpu.VMEM((8, 128, 256), bf16), pltpu.VMEM((256, 128), bf16), pltpu.VMEM((128, 256), bf16),
            pltpu.VMEM((8, 256), f32), pltpu.VMEM((128, 256), f32),
            pltpu.SemaphoreType.DMA((2,)), pltpu.SemaphoreType.DMA, pltpu.SemaphoreType.DMA((18,)), pltpu.SemaphoreType.DMA((18,)),
        ],
        compiler_params=pltpu.CompilerParams(vmem_limit_bytes=48 * 1024 * 1024),
        cost_estimate=pl.CostEstimate(flops=16_000_000_000, bytes_accessed=16_000_000, transcendentals=0),
    )(count, scale, slot, sel, got, packed, bias, conv, stem, head)


BOTH = ("grp", "dev")
COLUMNS = [[y * 8 + z * 2 + c for y in range(4) for c in range(2)] for z in range(4)]
ALONG_Z = [[y * 8 + z * 2 + c for z in range(4)] for y in range(4) for c in range(2)]


def prep_kernel(count_ref, req_ref, home_ref, maps_ref, heat_ref, asked_ref, sel_ref, mine_ref, wide):
    count = count_ref[0]
    wide[...] = maps_ref[...].reshape(512, 128).astype(f32)

    for p in range(64):
        mine_ref[0, :, p * 128:(p + 1) * 128] = wide[pl.ds(p, 8, stride=64), :].astype(bf16)
    mine_ref[0, :, 8192:9216] = heat_ref[...]
    for k in range(1, 4):
        mine_ref[k] = mine_ref[0]

    i = lax.broadcasted_iota(jnp.int32, (32, 32), 0)
    j = lax.broadcasted_iota(jnp.int32, (32, 32), 1)
    req = jnp.sum(jnp.where(i == j, req_ref[...], 0), axis=1, keepdims=True)
    lane = lax.broadcasted_iota(jnp.int32, (32, 256), 1)
    pos = jnp.sum(jnp.where(lane == req, home_ref[...], 0), axis=1, keepdims=True)
    owner = pos >> 3
    column = (owner >> 3) * 2 + (owner & 1)
    row = ((owner >> 1) & 3) * 8 + (pos & 7)
    across_lanes = jnp.sum(jnp.where(i == j, column, 0), axis=0, keepdims=True)
    live = lax.broadcasted_iota(jnp.int32, (32, 1), 0) < count
    earlier = (across_lanes == column) & (j < i) & (j < count)
    rank = jnp.minimum(jnp.sum(jnp.where(earlier, 1, 0), axis=1, keepdims=True), 7)
    lane64 = lax.broadcasted_iota(jnp.int32, (32, 64), 1)
    pick = jnp.where((lane64 == column * 8 + rank) & live, 1.0, 0.0)
    sel_ref[...] = pick.astype(bf16)
    value = jnp.broadcast_to((row + 1).astype(f32), (32, 128)).astype(bf16)
    asked = lax.dot_general(pick.astype(bf16), value, TN, preferred_element_type=f32)
    asked_ref[...] = (asked.astype(jnp.int32) - 1).reshape(8, 8, 128)


def prep(count, req, home, maps, heat):
    vm = pl.BlockSpec(memory_space=pltpu.VMEM)
    sm = pl.BlockSpec(memory_space=pltpu.SMEM)
    S = jax.ShapeDtypeStruct
    return pl.pallas_call(
        prep_kernel,
        out_shape=(S((8, 8, 128), jnp.int32), S((32, 64), bf16), S((4, 8, 9216), bf16)),
        in_specs=[sm, vm, vm, vm, vm],
        out_specs=(vm, vm, vm),
        scratch_shapes=[pltpu.VMEM((512, 128), f32)],
        compiler_params=pltpu.CompilerParams(vmem_limit_bytes=8 * 1024 * 1024),
    )(count, req, home, maps, heat)


def choose_kernel(table_ref, pile_ref, out_ref):
    lane = lax.broadcasted_iota(jnp.int32, (64, 32), 1)
    pick = jnp.where(table_ref[:, 0:32] == lane, 1.0, 0.0).astype(bf16)

    @pl.loop(0, 9)
    def _(k):
        out_ref[:, block(k, 1024)] = dot(pick, pile_ref[:, block(k, 1024)]).astype(bf16)


def choose(table, pile):
    vm = pl.BlockSpec(memory_space=pltpu.VMEM)
    return pl.pallas_call(
        choose_kernel,
        out_shape=jax.ShapeDtypeStruct((64, 9216), bf16),
        in_specs=[vm, vm],
        out_specs=vm,
        compiler_params=pltpu.CompilerParams(vmem_limit_bytes=8 * 1024 * 1024),
        cost_estimate=pl.CostEstimate(flops=40000000, bytes_accessed=2000000, transcendentals=0),
    )(table, pile)


PARTS = 4
PART = 4608 // PARTS


def pack_kernel(slot_ref, conv_hbm, stem_ref, head_ref, bias_ref, out_hbm, wide, narrow, isem, osem):
    def load(k):
        r = block(k, PART)
        return pltpu.make_async_copy(conv_hbm.at[r], wide.at[r], isem.at[k])

    def save(k):
        r = block(k, PART)
        return pltpu.make_async_copy(narrow.at[r], out_hbm.at[slot_ref[0], r], osem.at[k])

    for k in range(PARTS):
        load(k).start()
    narrow[4608:4736, :] = stem_ref[...].astype(bf16)
    narrow[4736:4752, :] = head_ref[...].astype(bf16)
    narrow[4752:4768, :] = jnp.concatenate([bias_ref[...], jnp.zeros((13, 256), f32)], axis=0).astype(bf16)
    last = pltpu.make_async_copy(
        narrow.at[pl.ds(4608, 160)], out_hbm.at[slot_ref[0], pl.ds(4608, 160)], osem.at[PARTS])
    last.start()

    @pl.loop(0, PARTS)
    def _(k):
        load(k).wait()

        @pl.loop(0, PART // 64)
        def _(q):
            r = pl.ds(pl.multiple_of(k * PART + q * 64, 64), 64)
            narrow[r, :] = wide[r, :].astype(bf16)

        save(k).start()

    for k in range(PARTS):
        save(k).wait()
    last.wait()


def pack(slot, conv, stem, head, bias):
    vm = pl.BlockSpec(memory_space=pltpu.VMEM)
    sm = pl.BlockSpec(memory_space=pltpu.SMEM)
    hb = pl.BlockSpec(memory_space=pltpu.HBM)
    return pl.pallas_call(
        pack_kernel,
        out_shape=jax.ShapeDtypeStruct((2, PACKED, 256), bf16),
        in_specs=[sm, hb, vm, vm, vm],
        out_specs=hb,
        scratch_shapes=[
            pltpu.VMEM((4608, 256), f32),
            pltpu.VMEM((PACKED, 256), bf16),
            pltpu.SemaphoreType.DMA((PARTS,)),
            pltpu.SemaphoreType.DMA((PARTS + 1,)),
        ],
        compiler_params=pltpu.CompilerParams(vmem_limit_bytes=16 * 1024 * 1024),
        cost_estimate=pl.CostEstimate(flops=1000000, bytes_accessed=7000000, transcendentals=0),
    )(slot, conv, stem, head, bias)


MIX = 8
PIECE = 4608 // MIX


def mix_kernel(slot_ref, t_hbm, base_hbm, bstem_ref, bhead_ref, bbias_ref, new_hbm, nstem_ref, nhead_ref, nbias_ref,
               theirs, wide, asem, bsem, osem):
    def loads(k):
        r = block(k, PIECE)
        return (pltpu.make_async_copy(t_hbm.at[slot_ref[0], r], theirs.at[r], asem.at[k]),
                pltpu.make_async_copy(base_hbm.at[r], wide.at[r], bsem.at[k]))

    def save(k):
        r = block(k, PIECE)
        return pltpu.make_async_copy(wide.at[r], new_hbm.at[r], osem.at[k])

    tail = pltpu.make_async_copy(t_hbm.at[slot_ref[0], pl.ds(4608, 160)], theirs.at[pl.ds(4608, 160)], asem.at[MIX])
    for k in range(MIX):
        for c in loads(k):
            c.start()
    tail.start()

    @pl.loop(0, MIX)
    def _(k):
        for c in loads(k):
            c.wait()

        @pl.loop(0, PIECE // 64)
        def _(q):
            r = pl.ds(pl.multiple_of(k * PIECE + q * 64, 64), 64)
            wide[r, :] = wide[r, :] + 0.5 * theirs[r, :].astype(f32)

        save(k).start()

    tail.wait()
    nstem_ref[...] = bstem_ref[...] + 0.5 * theirs[4608:4736, :].astype(f32)
    nhead_ref[...] = bhead_ref[...] + 0.5 * theirs[4736:4752, :].astype(f32)
    nbias_ref[...] = bbias_ref[...] + 0.5 * theirs[4752:4768, :].astype(f32)[0:3, :]
    for k in range(MIX):
        save(k).wait()


def mix(slot, theirs, base, bstem, bhead, bbias):
    vm = pl.BlockSpec(memory_space=pltpu.VMEM)
    sm = pl.BlockSpec(memory_space=pltpu.SMEM)
    hb = pl.BlockSpec(memory_space=pltpu.HBM)
    S = jax.ShapeDtypeStruct
    return pl.pallas_call(
        mix_kernel,
        out_shape=(S((4608, 256), f32), S((128, 256), f32), S((16, 256), f32), S((3, 256), f32)),
        in_specs=[sm, hb, hb, vm, vm, vm],
        out_specs=(hb, vm, vm, vm),
        scratch_shapes=[
            pltpu.VMEM((PACKED, 256), bf16),
            pltpu.VMEM((4608, 256), f32),
            pltpu.SemaphoreType.DMA((MIX + 1,)),
            pltpu.SemaphoreType.DMA((MIX,)),
            pltpu.SemaphoreType.DMA((MIX,)),
        ],
        compiler_params=pltpu.CompilerParams(vmem_limit_bytes=16 * 1024 * 1024),
        cost_estimate=pl.CostEstimate(flops=1000000, bytes_accessed=12000000, transcendentals=0),
    )(slot, theirs, base, bstem, bhead, bbias)


def swap(array, bit):
    pairs = [[i, i ^ (1 << bit)] for i in range(256) if not i >> bit & 1]
    return lax.all_to_all(array, BOTH, split_axis=0, concat_axis=0, axis_index_groups=pairs, tiled=True)


def among(array, groups):
    return lax.all_to_all(array, "dev", split_axis=0, concat_axis=0, axis_index_groups=groups, tiled=True)


def step(bit, counts, scale, slot, asked, sel, mine, packed, bias, conv, stem, head):
    if bit != 1:
        theirs = swap(packed, bit)
    pile = among(mine, ALONG_Z)
    table = among(asked, COLUMNS)
    if bit == 1:
        packed_late, pile, table = lax.optimization_barrier((packed, pile, table))
        theirs = swap(packed_late, bit)
    send = choose(table.reshape(64, 128), pile.reshape(32, 9216))
    got = among(send.reshape(8, 8, 9216), COLUMNS)
    outs = main_call(counts, scale, slot, sel, got.reshape(64, 9216), packed, bias, conv, stem, head)
    return (theirs, *outs)


def local(step_number, maps, heat, home, requests, counts, stem, conv, head, bias):
    bit = step_number % 8
    stem, conv, head, bias = stem[0], conv.reshape(4608, 256), head[0], bias[0]
    me = lax.axis_index("grp") * 32 + lax.axis_index("dev")
    slot = (1 - ((me >> bit) & 1)).astype(jnp.int32).reshape(1)
    scale = 2.0 / (counts.astype(f32) * 1024.0)
    packed = pack(slot, conv, stem, head, bias)
    asked, sel, mine = prep(counts, requests, home, maps, heat)
    outs = lax.switch(
        bit, [functools.partial(step, b) for b in range(8)],
        counts, scale, slot, asked, sel, mine, packed, bias, conv, stem, head,
    )
    theirs, gconv, base, gstem, ghead, gbias, bstem, bhead, bbias = outs
    new, nstem, nhead, nbias = mix(slot, theirs, base, bstem, bhead, bbias)
    return (
        nstem[None], new.reshape(1, 2, 2304, 256), nhead[None], nbias[None],
        gstem[None], gconv.reshape(1, 2, 2304, 256), ghead[None], gbias[None],
    )


def solution(mesh):
    placed = (
        P(),
        P(BOTH, None, None),
        P(BOTH, None),
        P("grp", None),
        P(BOTH, None),
        P(BOTH),
        P(BOTH, None, None),
        P(BOTH, None, None, None),
        P(BOTH, None, None),
        P(BOTH, None, None),
    )
    outs = (
        P(BOTH, None, None),
        P(BOTH, None, None, None),
        P(BOTH, None, None),
        P(BOTH, None, None),
        P(BOTH, None, None),
        P(BOTH, None, None, None),
        P(BOTH, None, None),
        P(BOTH, None, None),
    )
    return jax.shard_map(local, mesh=mesh, in_specs=placed, out_specs=outs, check_vma=False)
```

profile of v0, /device:TPU:1, one launch (start us, length us, event | category | flops | bytes accessed | tf_op | source)
XLA Modules:
  0.0 131.7 jit_solution(1991568855290999578)
XLA Ops:
  2.0 0.7 copy.21
  2.7 0.0 copy-start
  2.7 0.9 copy-done
  3.6 0.0 copy-start.1
  3.6 0.7 copy-done.1
  4.3 0.0 copy-start.2
  4.3 0.7 copy-done.2
  5.0 0.0 copy-start.3
  5.0 0.7 copy-done.3
  5.6 0.6 shard_map.162
  6.2 0.0 copy-start.4
  6.2 0.0 copy-start.5
  6.2 4.4 %shard_map.161 = bf16[2,4768,256]{2,1,0:T(8,128)(2,1)} custom-call(s32[1]{0:T(128)} %bitcast.32.slot_ref, f32[4608,256]{1,0:T(8,128)} %bitcast.80, f32[128,256]{1,0:T(8,128)} %bitcast.89, f32[16,256]{1,0:T(8,128)} %bitcast.98, f32[3,256]{1,0:T(4,128)S(1)} %bitcast.107), custom_call_target="tpu_custom_call" | custom-call | flops 1000000 | bytes 7000000 | tf_op jit(solution)/shard_map/pallas_call | solution.py:314
  10.6 0.0 copy-done.4
  10.6 0.0 copy-done.5
  10.6 114.7 %conditional.1 = (bf16[2,4768,256]{2,1,0:T(8,128)(2,1)}, bf16[4608,256]{1,0:T(8,128)(2,1)}, f32[4608,256]{1,0:T(8,128)}, bf16[128,256]{1,0:T(8,128)(2,1)}, bf16[...) conditional(s32[]{:T(128)} %clamp.3, ...), branch_computations={%region_0.1_spmd, %region_1.2_spmd, %region_2.3_spmd, %region_3.4_... | conditional | flops 16039999488 | bytes 36251880 | solution.py:424
  10.8 10.5 %all_to_all.140 = s32[8,8,128]{2,1,0:T(8,128)S(1)} all-to-all(s32[8,8,128]{2,1,0:T(8,128)S(1)} %get-tuple-element.260), channel_id=1, replica_groups={{0,1,8,9,16,17,24,25},{2,3,10,11,18,19,26,27},{4,5,12,13,20,21,28,29},{..., dimensions={0} | all-to-all | bytes 65536 | tf_op jit(solution)/shard_map/cond/branch_4_fun/all_to_all | solution.py:399
  21.3 20.7 %all_to_all.141 = bf16[4,8,9216]{2,1,0:T(8,128)(2,1)S(1)} all-to-all(bf16[4,8,9216]{2,1,0:T(8,128)(2,1)S(1)} %get-tuple-element.261), channel_id=1, replica_groups={{0,2,4,6},{1,3,5,7},{8,10,12,14},{9,11,13,15},{16,18,20,22},{17,19,21,2..., dimensions={0} | all-to-all | bytes 1179648 | tf_op jit(solution)/shard_map/cond/branch_4_fun/all_to_all | solution.py:399
  42.0 1.5 %branch_4_fun.2 = bf16[64,9216]{1,0:T(8,128)(2,1)S(1)} custom-call(s32[64,128]{1,0:T(8,128)S(1)} %bitcast.75, bf16[32,9216]{1,0:T(8,128)(2,1)S(1)} %bitcast.59), custom_call_target="tpu_custom_call" | custom-call | flops 40000000 | bytes 2000000 | tf_op jit(solution)/shard_map/cond/branch_4_fun/pallas_call | solution.py:262
  43.5 20.5 %all_to_all.142 = bf16[8,8,9216]{2,1,0:T(8,128)(2,1)S(1)} all-to-all(bf16[8,8,9216]{2,1,0:T(8,128)(2,1)S(1)} %bitcast.51), channel_id=1, replica_groups={{0,1,8,9,16,17,24,25},{2,3,10,11,18,19,26,27},{4,5,12,13,20,21,28,29},{..., dimensions={0} | all-to-all | bytes 2359296 | tf_op jit(solution)/shard_map/cond/branch_4_fun/all_to_all | solution.py:399
  63.9 5.8 %all-to-all-start.16 = ((bf16[2,4768,256]{2,1,0:T(8,128)(2,1)}), bf16[2,4768,256]{2,1,0:T(8,128)(2,1)}, u32[]{:S(2)}, u32[]{:S(2)}) async-start(bf16[2,4768,256]{2,1,0:T(8,128)(2,1)} %get-tuple-element.255.w_hbm), calls=%async_computation.16 | async-start | bytes 9764864 | tf_op jit(solution)/shard_map/cond/branch_4_fun/all_to_all | solution.py:395
  69.8 33.2 %branch_4_fun.3 = (bf16[4608,256]{1,0:T(8,128)(2,1)}, f32[4608,256]{1,0:T(8,128)}, bf16[128,256]{1,0:T(8,128)(2,1)}, bf16[16,256]{1,0:T(8,128)(2,1)}, bf16[3,256...) custom-call(s32[1]{0:T(128)} %get-tuple-element.256.count_ref, ...), custom_call_target="tpu_custom_call" | custom-call | flops 16000000000 | bytes 16000000 | tf_op jit(solution)/shard_map/cond/branch_4_fun/pallas_call | solution.py:184
  103.0 22.3 %all-to-all-done.16 = bf16[2,4768,256]{2,1,0:T(8,128)(2,1)} async-done(((bf16[2,4768,256]{2,1,0:T(8,128)(2,1)}), bf16[2,4768,256]{2,1,0:T(8,128)(2,1)}, u32[]{:S(2)}, u32[]{:S(2)}) %all-to-all-start.16) | async-done | bytes 4882464 | tf_op jit(solution)/shard_map/cond/branch_4_fun/all_to_all | solution.py:395
  125.3 5.9 %shard_map.163 = (f32[4608,256]{1,0:T(8,128)}, f32[128,256]{1,0:T(8,128)}, f32[16,256]{1,0:T(8,128)}, f32[3,256]{1,0:T(4,128)S(1)}) custom-call(s32[1]{0:T(128)} %bitcast.32.slot_ref, bf16[2,4768,256]{2,1,0:T(8,128)(2,1)} %get-tuple-element.358.t_hbm, f32[4608,256]{1,0:T(8,128)} %get-tuple-element.359.base_hbm, f32[128,256]{1,0:T(8,128)S(1)} %get-tuple-element.360.bstem_ref, ...), custom_call_target="tpu_custom_call" | custom-call | flops 1000000 | bytes 12000000 | tf_op jit(solution)/shard_map/pallas_call | solution.py:376
  131.1 0.6 copy.18
Async XLA Ops:
  2.7 0.9 copy-start
  3.6 0.7 copy-start.1
  4.3 0.7 copy-start.2
  5.0 0.7 copy-start.3
  6.2 4.4 %copy-start.4 = (f32[1,128,256]{2,1,0:T(8,128)S(1)}, f32[1,128,256]{2,1,0:T(8,128)}, u32[]{:S(2)}) copy-start(f32[1,128,256]{2,1,0:T(8,128)} %param.24) | copy-start | bytes 393220
  6.2 4.4 %copy-start.5 = (f32[1,16,256]{2,1,0:T(8,128)S(1)}, f32[1,16,256]{2,1,0:T(8,128)}, u32[]{:S(2)}) copy-start(f32[1,16,256]{2,1,0:T(8,128)} %param.26) | copy-start | bytes 49156
  63.9 61.3 %all-to-all-start.16 = ((bf16[2,4768,256]{2,1,0:T(8,128)(2,1)}), bf16[2,4768,256]{2,1,0:T(8,128)(2,1)}, u32[]{:S(2)}, u32[]{:S(2)}) async-start(bf16[2,4768,256]{2,1,0:T(8,128)(2,1)} %get-tuple-element.255.w_hbm), calls=%async_computation.16 | async-start | bytes 9764864 | tf_op jit(solution)/shard_map/cond/branch_4_fun/all_to_all | solution.py:395
where the time goes:
time: 132 us
  blocking collectives  51.7 us (39%)
  Pallas kernels  45.4 us (34%)
  waiting for transfers between devices  22.3 us (17%)
  starting transfers between devices  5.8 us (4%)
  local copies, waits for them, and re-layouts  4.24 us (3%)
  between operations  2.05 us (2%)
    all_to_all x3, blocking collectives, among(): lax.all_to_all(array, 'dev', split_axis=0, concat_axis=0, axis_index_grou...  51.7 us
    pallas_call x1, Pallas kernels, main_call(): pl.pallas_call(functools.partial(main_kernel, U=U, UB=UB), out_shape=(S((...  33.2 us
    all_to_all x1, waiting for transfers between devices, swap(): lax.all_to_all(array, BOTH, split_axis=0, concat_axis=0, axis_index_group...  22.3 us
    pallas_call x1, Pallas kernels, mix(): pl.pallas_call(mix_kernel, out_shape=(S((4608, 256), f32), S((128, 256),...  5.86 us
    all_to_all x1, starting transfers between devices, swap(): lax.all_to_all(array, BOTH, split_axis=0, concat_axis=0, axis_index_group...  5.8 us
    pallas_call x1, Pallas kernels, pack(): pl.pallas_call(pack_kernel, out_shape=jax.ShapeDtypeStruct((2, PACKED, 25...  4.35 us
    unnamed x14, local copies, waits for them, and re-layouts  4.24 us
  transfers between devices with their start and end apart: 1, of which 1 were waited for; matrix products, arithmetic and copies ran while one was open for 0% of the time, Pallas kernels for 25%

commit v1 on v0

v1 whole, which is shorter than its diff:
```python
import functools

import jax
import jax.numpy as jnp
from jax import lax
from jax.experimental import pallas as pl
from jax.experimental.pallas import tpu as pltpu
from jax.sharding import PartitionSpec as P


bf16 = jnp.bfloat16
f32 = jnp.float32
NT = (((1,), (1,)), ((), ()))
TN = (((0,), (0,)), ((), ()))
ROW_STEM = 4608
ROW_HEAD = 4736
PACKED = 4768


def dot(a, b):
    return jnp.dot(a, b, preferred_element_type=f32)


def block(i, n):
    return pl.ds(pl.multiple_of(i * n, n), n)


def main_kernel(
    count_ref, scale_ref, sel_ref, got_ref, w_hbm, bias_ref, conv_hbm, stem_ref, head_ref,
    gconv_hbm, base_hbm, gstem_ref, ghead_ref, gbias_ref,
    wb, mine, gb, x_s, heat_s, act, act_t, grad, whe, err_s, err_t, bsum, gstem_acc,
    tail, wsem, msem, tsem, osem, gsem, *, U, UB):
    wcopies = []
    for k, (lo, n) in enumerate(((ROW_STEM, PACKED - ROW_STEM), (0, ROW_STEM))):
        c = pltpu.make_async_copy(w_hbm.at[pl.ds(lo, n)], wb.at[pl.ds(lo, n)], wsem.at[k])
        c.start()
        wcopies.append(c)
    load_mine = pltpu.make_async_copy(conv_hbm, mine, msem)
    load_mine.start()

    edge = jnp.zeros((32, 256), bf16)

    @pl.loop(0, 10)
    def _(q):
        for buf, ks in ((act, (0, 1)), (grad, (1, 2))):
            for k in ks:
                buf[k, 0, block(q, 32), :] = edge
                buf[k, 9, block(q, 32), :] = edge
                buf[k, q, 0:32, :] = edge
                buf[k, q, 288:320, :] = edge

    @pl.loop(0, 6)
    def _(q):
        z = jnp.zeros((256, 256), bf16)
        act_t[q // 3, q % 3, :, 0:256] = z
        act_t[q // 3, q % 3, :, 2304:2560] = z

    sel = sel_ref[...]
    wcopies[0].wait()
    ws = wb[ROW_STEM:ROW_STEM + 128, :]
    b0 = bias_ref[0]

    @pl.loop(0, 8)
    def _(u):
        r = dot(sel, got_ref[:, block(u, 1024)]).astype(bf16)
        x = jnp.concatenate([r[:, v * 128:(v + 1) * 128] for v in range(8)], axis=0)
        x_s[u] = x
        heat_s[block(u, 32), :] = dot(sel, got_ref[:, pl.ds(pl.multiple_of(8192 + u * 128, 128), 128)])
        pre = dot(x, ws) + b0
        a = jnp.maximum(pre, 0.0).astype(bf16)
        act[0, u + 1, 32:288, :] = a

    wcopies[1].wait()
    n = 8 // U

    @pl.loop(0, 2 * n)
    def _(k):
        s = k // n
        u = (k - s * n) * U
        rows = []
        for e in range(U):
            rows.append(jnp.concatenate(
                [act[s, u + e + i, j * 32:j * 32 + 256, :] for i in range(3) for j in range(3)], axis=1))
        lhs = rows[0] if U == 1 else jnp.concatenate(rows, axis=0)
        pre = dot(lhs, wb[block(s, 2304), :]) + bias_ref[s + 1]
        for e in range(U):
            for j in range(3):
                act_t[s, j, :, block(u + e + 1, 256)] = act[s, u + e + 1, j * 32:j * 32 + 256, :].T
        keep = s.astype(f32)
        for e in range(U):
            p = pre[e * 256:(e + 1) * 256] + keep * act[0, u + e + 1, 32:288, :].astype(f32)
            a = jnp.maximum(p, 0.0).astype(bf16)
            act[s + 1, u + e + 1, 32:288, :] = a

    count = count_ref[0]
    scale = scale_ref[0]
    wh = wb[ROW_HEAD:ROW_HEAD + 16, :]

    def predict(v, pred):
        whe[v] = jnp.zeros((128, 256), bf16)
        whe[v, block(v, 16), :] = wh
        a = act[2, 1:9, pl.ds(pl.multiple_of(v * 32 + 32, 32), 32), :].reshape(256, 256)
        return pred + lax.dot_general(a, whe[v], NT, preferred_element_type=f32)

    pred = lax.fori_loop(0, 8, predict, jnp.zeros((256, 128), f32))
    row = lax.broadcasted_iota(jnp.int32, (256, 128), 0)
    err = jnp.where((row & 31) < count, (pred - heat_s[...]) * scale, 0.0).astype(bf16)
    err_s[...] = err
    err_t[...] = err.T
    bsum[...] = jnp.zeros_like(bsum)

    def spread(v, gh):
        at = pl.ds(pl.multiple_of(v * 32 + 32, 32), 32)
        a = act[2, 1:9, at, :].reshape(256, 256)
        d = jnp.where(a > 0, dot(err_s[...], whe[v]), 0.0).astype(bf16)
        bsum[2:3, :] += jnp.sum(d.astype(f32), axis=0, keepdims=True)
        grad[2, 1:9, at, :] = d.reshape(8, 32, 256)
        return gh + dot(err_t[block(v, 16), :], a)

    gh = lax.fori_loop(0, 8, spread, jnp.zeros((16, 256), f32))
    ghead_ref[...] = gh.astype(bf16)
    tail[128:144, :] = 0.5 * head_ref[...] - 0.1 * gh

    m = 8 // UB

    @pl.loop(0, 2 * m)
    def _(k):
        q = k // m
        s = 1 - q
        u = (k - q * m) * UB
        da = None
        for i in range(3):
            for j in range(3):
                ii, jj = 2 - i, 2 - j
                rows = [grad[s + 1, u + e + ii, jj * 32:jj * 32 + 256, :] for e in range(UB)]
                lhs = rows[0] if UB == 1 else jnp.concatenate(rows, axis=0)
                w = wb[pl.ds(pl.multiple_of(s * 2304 + (3 * i + j) * 256, 256), 256), :]
                t = lax.dot_general(lhs, w, NT, preferred_element_type=f32)
                da = t if da is None else da + t
        keep = q.astype(f32)
        for e in range(UB):
            d = da[e * 256:(e + 1) * 256] + keep * grad[2, u + e + 1, 32:288, :].astype(f32)
            d = jnp.where(act[s, u + e + 1, 32:288, :] > 0, d, 0.0).astype(bf16)
            grad[s, u + e + 1, 32:288, :] = d
            bsum[pl.ds(s, 1), :] += jnp.sum(d.astype(f32), axis=0, keepdims=True)

    gbias_ref[...] = bsum[0:3, :].astype(bf16)
    tail[144:152, :] = 0.5 * jnp.concatenate([bias_ref[0], bias_ref[1], bias_ref[2], jnp.zeros((5, 256), f32)], axis=0) - 0.1 * bsum[...]
    tail[152:160, :] = jnp.zeros((8, 256), f32)
    gstem_acc[...] = jnp.zeros_like(gstem_acc)

    @pl.loop(0, 8)
    def _(u):
        gstem_acc[...] += lax.dot_general(x_s[u], grad[0, u + 1, 32:288, :], TN, preferred_element_type=f32)

    gs = gstem_acc[...]
    gstem_ref[...] = gs.astype(bf16)
    tail[0:128, :] = 0.5 * stem_ref[...] - 0.1 * gs
    save_tail = pltpu.make_async_copy(tail, base_hbm.at[pl.ds(ROW_STEM, 160)], tsem)
    save_tail.start()

    load_mine.wait()

    def outs(t):
        r = block(t, 256)
        return (pltpu.make_async_copy(gb.at[r], gconv_hbm.at[r], gsem.at[t]),
                pltpu.make_async_copy(mine.at[r], base_hbm.at[r], osem.at[t]))

    @pl.loop(0, 6)
    def _(q):
        s = q // 3
        j = q - s * 3
        rhs = grad[s + 1, 1:9, 32:288, :].reshape(2048, 256)
        lhs = jnp.concatenate([act_t[s, j, :, i * 256:i * 256 + 2048] for i in range(3)], axis=0)
        all_rows = dot(lhs, rhs)
        for i in range(3):
            t = s * 9 + i * 3 + j
            g = all_rows[i * 256:(i + 1) * 256]
            r = block(t, 256)
            gb[r, :] = g.astype(bf16)
            mine[r, :] = 0.5 * mine[r, :] - 0.1 * g
            for c in outs(t):
                c.start()

    @pl.loop(0, 18)
    def _(t):
        for c in outs(t):
            c.wait()

    save_tail.wait()


def main_call(count, scale, sel, got, packed, bias, conv, stem, head, U=4, UB=2):
    vm = pl.BlockSpec(memory_space=pltpu.VMEM)
    sm = pl.BlockSpec(memory_space=pltpu.SMEM)
    hb = pl.BlockSpec(memory_space=pltpu.HBM)
    S = jax.ShapeDtypeStruct
    maps = pltpu.VMEM((3, 10, 320, 256), bf16)
    return pl.pallas_call(
        functools.partial(main_kernel, U=U, UB=UB),
        out_shape=(S((4608, 256), bf16), S((PACKED, 256), f32), S((128, 256), bf16), S((16, 256), bf16), S((3, 256), bf16)),
        in_specs=[sm, sm, vm, vm, hb, vm, hb, vm, vm],
        out_specs=(hb, hb, vm, vm, vm),
        scratch_shapes=[
            pltpu.VMEM((PACKED, 256), bf16), pltpu.VMEM((4608, 256), f32), pltpu.VMEM((4608, 256), bf16),
            pltpu.VMEM((8, 256, 128), bf16), pltpu.VMEM((256, 128), f32), maps, pltpu.VMEM((2, 3, 256, 2560), bf16), maps,
            pltpu.VMEM((8, 128, 256), bf16), pltpu.VMEM((256, 128), bf16), pltpu.VMEM((128, 256), bf16),
            pltpu.VMEM((8, 256), f32), pltpu.VMEM((128, 256), f32), pltpu.VMEM((160, 256), f32),
            pltpu.SemaphoreType.DMA((2,)), pltpu.SemaphoreType.DMA, pltpu.SemaphoreType.DMA, pltpu.SemaphoreType.DMA((18,)), pltpu.SemaphoreType.DMA((18,)),
        ],
        compiler_params=pltpu.CompilerParams(vmem_limit_bytes=48 * 1024 * 1024),
        cost_estimate=pl.CostEstimate(flops=16_000_000_000, bytes_accessed=16_000_000, transcendentals=0),
    )(count, scale, sel, got, packed, bias, conv, stem, head)


BOTH = ("grp", "dev")
COLUMNS = [[y * 8 + z * 2 + c for y in range(4) for c in range(2)] for z in range(4)]


def prep_kernel(count_ref, zpos_ref, req_hbm, home_hbm, maps_hbm, heat_hbm, asked_ref, sel_ref, mine_ref, req, home, heat, maps, wide, sems):
    copies = [
        pltpu.make_async_copy(src, dst, sems.at[k])
        for k, (src, dst) in enumerate(((maps_hbm, maps), (heat_hbm, heat), (req_hbm, req), (home_hbm, home)))
    ]
    for c in copies:
        c.start()
    count = count_ref[0]
    copies[2].wait()
    copies[3].wait()
    i = lax.broadcasted_iota(jnp.int32, (32, 32), 0)
    j = lax.broadcasted_iota(jnp.int32, (32, 32), 1)
    wanted = jnp.sum(jnp.where(i == j, req[...], 0), axis=1, keepdims=True)
    lane = lax.broadcasted_iota(jnp.int32, (32, 256), 1)
    pos = jnp.sum(jnp.where(lane == wanted, home[...], 0), axis=1, keepdims=True)
    owner = pos >> 3
    column = (owner >> 3) * 2 + (owner & 1)
    row = (((owner >> 1) & 3) ^ zpos_ref[0]) * 8 + (pos & 7)
    across_lanes = jnp.sum(jnp.where(i == j, column, 0), axis=0, keepdims=True)
    live = lax.broadcasted_iota(jnp.int32, (32, 1), 0) < count
    earlier = (across_lanes == column) & (j < i) & (j < count)
    rank = jnp.minimum(jnp.sum(jnp.where(earlier, 1, 0), axis=1, keepdims=True), 7)
    lane64 = lax.broadcasted_iota(jnp.int32, (32, 64), 1)
    pick = jnp.where((lane64 == column * 8 + rank) & live, 1.0, 0.0)
    sel_ref[...] = pick.astype(bf16)
    value = jnp.broadcast_to((row + 1).astype(f32), (32, 128)).astype(bf16)
    asked = lax.dot_general(pick.astype(bf16), value, TN, preferred_element_type=f32)
    asked_ref[...] = (asked.astype(jnp.int32) - 1).reshape(8, 8, 128)
    copies[0].wait()
    wide[...] = maps[...].reshape(512, 128).astype(f32)
    for p in range(64):
        mine_ref[:, p * 128:(p + 1) * 128] = wide[pl.ds(p, 8, stride=64), :].astype(bf16)
    copies[1].wait()
    mine_ref[:, 8192:9216] = heat[...]


def prep(count, zpos, req, home, maps, heat):
    vm = pl.BlockSpec(memory_space=pltpu.VMEM)
    sm = pl.BlockSpec(memory_space=pltpu.SMEM)
    hb = pl.BlockSpec(memory_space=pltpu.HBM)
    S = jax.ShapeDtypeStruct
    return pl.pallas_call(
        prep_kernel,
        out_shape=(S((8, 8, 128), jnp.int32), S((32, 64), bf16), S((8, 9216), bf16)),
        in_specs=[sm, sm, hb, hb, hb, hb],
        out_specs=(vm, vm, vm),
        scratch_shapes=[
            pltpu.VMEM((1, 32), jnp.int32),
            pltpu.VMEM((1, 256), jnp.int32),
            pltpu.VMEM((8, 1024), bf16),
            pltpu.VMEM((8, 64, 128), bf16),
            pltpu.VMEM((512, 128), f32),
            pltpu.SemaphoreType.DMA((4,)),
        ],
        compiler_params=pltpu.CompilerParams(vmem_limit_bytes=60 * 1024 * 1024),
    )(count, zpos, req, home, maps, heat)


def choose_kernel(table_ref, *refs):
    *piles, out_ref = refs
    lane = lax.broadcasted_iota(jnp.int32, (64, 32), 1)
    pick = jnp.where(table_ref[:, 0:32] == lane, 1.0, 0.0).astype(bf16)

    @pl.loop(0, 9)
    def _(k):
        pile = jnp.concatenate([p[:, block(k, 1024)] for p in piles], axis=0)
        out_ref[:, block(k, 1024)] = dot(pick, pile).astype(bf16)


def choose(table, *piles):
    vm = pl.BlockSpec(memory_space=pltpu.VMEM)
    return pl.pallas_call(
        choose_kernel,
        out_shape=jax.ShapeDtypeStruct((64, 9216), bf16),
        in_specs=[vm] * 5,
        out_specs=vm,
        compiler_params=pltpu.CompilerParams(vmem_limit_bytes=8 * 1024 * 1024),
        cost_estimate=pl.CostEstimate(flops=40000000, bytes_accessed=2000000, transcendentals=0),
    )(table, *piles)


PARTS = 6
PART = 4608 // PARTS


def pack_kernel(conv_hbm, stem_hbm, head_hbm, bias_hbm, out_hbm, wide, bias, narrow, isem, osem):
    def load(k):
        r = block(k, PART)
        return pltpu.make_async_copy(conv_hbm.at[r], wide.at[r], isem.at[k])

    def save(k):
        r = block(k, PART)
        return pltpu.make_async_copy(narrow.at[r], out_hbm.at[r], osem.at[k])

    def save_tail():
        r = pl.ds(ROW_STEM, 160)
        return pltpu.make_async_copy(narrow.at[r], out_hbm.at[r], osem.at[PARTS])

    small = [
        pltpu.make_async_copy(stem_hbm, wide.at[pl.ds(ROW_STEM, 128)], isem.at[PARTS]),
        pltpu.make_async_copy(head_hbm, wide.at[pl.ds(ROW_HEAD, 16)], isem.at[PARTS + 1]),
        pltpu.make_async_copy(bias_hbm, bias, isem.at[PARTS + 2]),
    ]
    for k in range(PARTS):
        load(k).start()
    for c in small:
        c.start()

    def narrowed(lo, n):
        @pl.loop(0, n // 48)
        def _(q):
            r = pl.ds(pl.multiple_of(lo + q * 48, 16), 48)
            narrow[r, :] = wide[r, :].astype(bf16)

    @pl.loop(0, PARTS)
    def _(k):
        load(k).wait()
        narrowed(k * PART, PART)
        save(k).start()

    for c in small:
        c.wait()
    narrowed(ROW_STEM, 144)
    narrow[ROW_STEM + 144:PACKED, :] = jnp.concatenate([bias[0], bias[1], bias[2], jnp.zeros((13, 256), f32)], axis=0).astype(bf16)
    save_tail().start()

    @pl.loop(0, PARTS)
    def _(k):
        save(k).wait()

    save_tail().wait()


def pack(conv, stem, head, bias):
    hb = pl.BlockSpec(memory_space=pltpu.HBM)
    return pl.pallas_call(
        pack_kernel,
        out_shape=jax.ShapeDtypeStruct((PACKED, 256), bf16),
        in_specs=[hb, hb, hb, hb],
        out_specs=hb,
        scratch_shapes=[
            pltpu.VMEM((PACKED, 256), f32),
            pltpu.VMEM((3, 1, 256), f32),
            pltpu.VMEM((PACKED, 256), bf16),
            pltpu.SemaphoreType.DMA((PARTS + 3,)),
            pltpu.SemaphoreType.DMA((PARTS + 1,)),
        ],
        compiler_params=pltpu.CompilerParams(vmem_limit_bytes=16 * 1024 * 1024),
        cost_estimate=pl.CostEstimate(flops=1000000, bytes_accessed=7000000, transcendentals=0),
    )(conv, stem, head, bias)


MIX = 8
PIECE = 4608 // MIX


def mix_kernel(t_hbm, base_hbm, new_hbm, nstem_hbm, nhead_hbm, nbias_ref, theirs, wide, asem, bsem, osem):
    def loads(k, r):
        return (pltpu.make_async_copy(t_hbm.at[r], theirs.at[r], asem.at[k]),
                pltpu.make_async_copy(base_hbm.at[r], wide.at[r], bsem.at[k]))

    def save(k):
        r = block(k, PIECE)
        return pltpu.make_async_copy(wide.at[r], new_hbm.at[r], osem.at[k])

    last = loads(MIX, pl.ds(ROW_STEM, 160))
    for c in last:
        c.start()
    for k in range(MIX):
        for c in loads(k, block(k, PIECE)):
            c.start()

    def mixed(lo, n):
        @pl.loop(0, n // 32)
        def _(q):
            r = pl.ds(pl.multiple_of(lo + q * 32, 32), 32)
            wide[r, :] = wide[r, :] + 0.5 * theirs[r, :].astype(f32)

    for c in last:
        c.wait()
    mixed(ROW_STEM, 160)
    small = (pltpu.make_async_copy(wide.at[pl.ds(ROW_STEM, 128)], nstem_hbm, osem.at[MIX]),
             pltpu.make_async_copy(wide.at[pl.ds(ROW_HEAD, 16)], nhead_hbm, osem.at[MIX + 1]))
    for c in small:
        c.start()
    for k in range(3):
        nbias_ref[k] = wide[ROW_HEAD + 16 + k:ROW_HEAD + 17 + k, :]

    @pl.loop(0, MIX)
    def _(k):
        for c in loads(k, block(k, PIECE)):
            c.wait()
        mixed(k * PIECE, PIECE)
        save(k).start()

    @pl.loop(0, MIX)
    def _(k):
        save(k).wait()

    for c in small:
        c.wait()


def mix(theirs, base):
    vm = pl.BlockSpec(memory_space=pltpu.VMEM)
    hb = pl.BlockSpec(memory_space=pltpu.HBM)
    S = jax.ShapeDtypeStruct
    return pl.pallas_call(
        mix_kernel,
        out_shape=(S((4608, 256), f32), S((128, 256), f32), S((16, 256), f32), S((3, 1, 256), f32)),
        in_specs=[hb, hb],
        out_specs=(hb, hb, hb, vm),
        scratch_shapes=[
            pltpu.VMEM((PACKED, 256), bf16),
            pltpu.VMEM((PACKED, 256), f32),
            pltpu.SemaphoreType.DMA((MIX + 1,)),
            pltpu.SemaphoreType.DMA((MIX + 1,)),
            pltpu.SemaphoreType.DMA((MIX + 2,)),
        ],
        compiler_params=pltpu.CompilerParams(vmem_limit_bytes=16 * 1024 * 1024),
        cost_estimate=pl.CostEstimate(flops=1000000, bytes_accessed=12000000, transcendentals=0),
    )(theirs, base)


def swap(array, bit):
    return lax.ppermute(array, BOTH, [(i, i ^ (1 << bit)) for i in range(256)])


def along_z(array, mask):
    return lax.ppermute(array, "dev", [(i, i ^ (mask << 1)) for i in range(32)])


def among(array):
    return lax.all_to_all(array, "dev", split_axis=0, concat_axis=0, axis_index_groups=COLUMNS, tiled=True)


def step(bit, counts, scale, sel, send, packed, bias, conv, stem, head):
    theirs = swap(packed, bit)
    got = among(send)
    outs = main_call(counts, scale, sel, got.reshape(64, 9216), packed, bias, conv, stem, head)
    return (theirs, *outs)


def local(step_number, maps, heat, home, requests, counts, stem, conv, head, bias):
    stem, conv, head, bias = stem[0], conv.reshape(4608, 256), head[0], jnp.transpose(bias, (1, 0, 2))
    zpos = ((lax.axis_index("dev") >> 1) & 3).astype(jnp.int32).reshape(1)
    scale = 2.0 / (counts.astype(f32) * 1024.0)
    asked, sel, mine = prep(counts, zpos, requests, home, maps, heat)
    others = [along_z(mine, mask) for mask in (1, 2, 3)]
    table = among(asked)
    packed = pack(conv, stem, head, bias)
    send = choose(table.reshape(64, 128), mine, *others)
    outs = lax.switch(
        step_number % 8, [functools.partial(step, b) for b in range(8)],
        counts, scale, sel, send.reshape(8, 8, 9216), packed, bias, conv, stem, head,
    )
    theirs, gconv, base, gstem, ghead, gbias = outs
    new, nstem, nhead, nbias = mix(theirs, base)
    return (
        nstem[None], new.reshape(1, 2, 2304, 256), nhead[None], jnp.transpose(nbias, (1, 0, 2)),
        gstem[None], gconv.reshape(1, 2, 2304, 256), ghead[None], gbias[None],
    )


def solution(mesh):
    placed = (
        P(),
        P(BOTH, None, None),
        P(BOTH, None),
        P("grp", None),
        P(BOTH, None),
        P(BOTH),
        P(BOTH, None, None),
        P(BOTH, None, None, None),
        P(BOTH, None, None),
        P(BOTH, None, None),
    )
    outs = (
        P(BOTH, None, None),
        P(BOTH, None, None, None),
        P(BOTH, None, None),
        P(BOTH, None, None),
        P(BOTH, None, None),
        P(BOTH, None, None, None),
        P(BOTH, None, None),
        P(BOTH, None, None),
    )
    return jax.shard_map(local, mesh=mesh, in_specs=placed, out_specs=outs, check_vma=False)
```

time: 132 us -> 103 us (0.78)
  blocking collectives: 51.7 us -> 0 us
  waiting for transfers between devices: 22.3 us -> 37.1 us
  starting transfers between devices: 5.8 us -> 20 us
  local copies, waits for them, and re-layouts: 4.24 us -> 0.03 us
  Pallas kernels: 45.4 us -> 42.7 us
    all_to_all x3 -> x0, blocking collectives: 51.7 us -> none  [among(): lax.all_to_all(array, 'dev', split_axis=0, concat_axis=0, axis_index_grou...]
    ppermute x0 -> x4, waiting for transfers between devices: none -> 23.3 us  [the longest x1 22.4 us: swap(): return lax.ppermute(array, BOTH, [(i, i ^ 1 << bit) for i in range(256)])]
    ppermute x0 -> x4, starting transfers between devices: none -> 8.49 us  [the longest x3 5.63 us: along_z(): return lax.ppermute(array, 'dev', [(i, i ^ mask << 1) for i in range(32)])]
    all_to_all x1 -> x2, waiting for transfers between devices: 22.3 us -> 13.8 us  [among(): lax.all_to_all(array, 'dev', split_axis=0, concat_axis=0, axis_index_grou...]
    all_to_all x1 -> x2, starting transfers between devices: 5.8 us -> 11.5 us  [among(): lax.all_to_all(array, 'dev', split_axis=0, concat_axis=0, axis_index_grou...]
    unnamed x14 -> x8, local copies, waits for them, and re-layouts: 4.24 us -> 0.03 us
    pallas_call x1, Pallas kernels: 33.2 us -> 30.1 us  [main_call(): pl.pallas_call(functools.partial(main_kernel, U=U, UB=UB), out_shape=(S((...]
    pallas_call x1, Pallas kernels: 0.55 us -> 2.11 us  [prep(): pl.pallas_call(prep_kernel, out_shape=(S((8, 8, 128), jnp.int32), S((32,...]
  transfers between devices with their start and end apart: 1 -> 6, of which waited for: 1 -> 4; matrix products, arithmetic and copies ran while one was open for 0% -> 0% of each run, Pallas kernels for 25% -> 33%
where the time goes in v1:
time: 103 us; the launch traced here: 102 us
  Pallas kernels  42.7 us (41%)
  waiting for transfers between devices  37.1 us (36%)
  starting transfers between devices  20 us (19%)
  between operations  2.27 us (2%)
    pallas_call x1, Pallas kernels, main_call(): pl.pallas_call(functools.partial(main_kernel, U=U, UB=UB), out_shape=(S((...  30.1 us
    ppermute x1, waiting for transfers between devices, swap(): return lax.ppermute(array, BOTH, [(i, i ^ 1 << bit) for i in range(256)])  22.4 us
    all_to_all x2, waiting for transfers between devices, among(): lax.all_to_all(array, 'dev', split_axis=0, concat_axis=0, axis_index_grou...  13.8 us
    all_to_all x2, starting transfers between devices, among(): lax.all_to_all(array, 'dev', split_axis=0, concat_axis=0, axis_index_grou...  11.5 us
    ppermute x3, starting transfers between devices, along_z(): return lax.ppermute(array, 'dev', [(i, i ^ mask << 1) for i in range(32)])  5.63 us
    pallas_call x1, Pallas kernels, mix(): pl.pallas_call(mix_kernel, out_shape=(S((4608, 256), f32), S((128, 256),...  4.37 us
    pallas_call x1, Pallas kernels, pack(): pl.pallas_call(pack_kernel, out_shape=jax.ShapeDtypeStruct((PACKED, 256),...  3.68 us
    ppermute x1, starting transfers between devices, swap(): return lax.ppermute(array, BOTH, [(i, i ^ 1 << bit) for i in range(256)])  2.86 us
  transfers between devices with their start and end apart: 6, of which 4 were waited for; matrix products, arithmetic and copies ran while one was open for 0% of the time, Pallas kernels for 33%

profile of v1, /device:TPU:1, one launch (start us, length us, event | category | flops | bytes accessed | tf_op | source)
XLA Modules:
  0.0 102.4 jit_solution(10309947564942944061)
XLA Ops:
  1.3 2.1 %shard_map.162 = (s32[8,8,128]{2,1,0:T(8,128)}, bf16[32,64]{1,0:T(8,128)(2,1)S(1)}, bf16[8,9216]{1,0:T(8,128)(2,1)}) custom-call(s32[1]{0:T(128)S(6)} %copy.67.count_ref, s32[1]{0:T(128)} %bitcast.12.zpos_ref, s32[1,32]{1,0:T(1,128)} %req_hbm.1, s32[1,256]{1,0:T(1,128)} %home_hbm.1, bf16[8,64,128]{2,1,0:T(8,128)(2,1)} %maps_hbm.1, bf16[8,1024]{1,0:T(8,128)(2,1)} %heat_hbm.1), custom_call_target="tpu_custom_call" | custom-call | tf_op jit(solution)/shard_map/pallas_call | solution.py:261
  3.4 5.2 %collective-permute-start.10 = (bf16[8,9216]{1,0:T(8,128)(2,1)}, bf16[8,9216]{1,0:T(8,128)(2,1)S(1)}, u32[]{:S(2)}, u32[]{:S(2)}) collective-permute-start(bf16[8,9216]{1,0:T(8,128)(2,1)} %get-tuple-element.278.refs_0_), channel_id=1, source_target_pairs={{0,6},{1,7},{2,4},{3,5},{4,2},{5,3},{6,0},{7,1},{8,14},{9,15},{10,... | collective-permute-start | bytes 442376 | tf_op jit(solution)/shard_map/ppermute | solution.py:449
  8.7 0.0 collective-permute-start.9
  8.7 0.4 collective-permute-start.8
  9.0 5.7 %all-to-all-start.8 = ((s32[8,8,128]{2,1,0:T(8,128)}), s32[8,8,128]{2,1,0:T(8,128)S(1)}, u32[]{:S(2)}, u32[]{:S(2)}) async-start(s32[8,8,128]{2,1,0:T(8,128)} %get-tuple-element.277), calls=%async_computation.8 | async-start | bytes 65536 | tf_op jit(solution)/shard_map/all_to_all | solution.py:453
  15.5 0.0 copy-start
  15.5 0.0 copy-start.1
  15.5 0.0 copy-start.2
  15.5 0.0 copy-start.3
  15.5 3.7 %shard_map.161 = bf16[4768,256]{1,0:T(8,128)(2,1)} custom-call(f32[4608,256]{1,0:T(8,128)} %bitcast.32, f32[128,256]{1,0:T(8,128)} %bitcast.41, f32[16,256]{1,0:T(8,128)} %bitcast.50, f32[3,1,256]{2,1,0:T(1,128)} %bitcast.59), custom_call_target="tpu_custom_call" | custom-call | flops 1000000 | bytes 7000000 | tf_op jit(solution)/shard_map/pallas_call | solution.py:355
  19.2 0.3 all-to-all-done.8
  19.5 0.0 collective-permute-done.10.refs_3_
  19.5 1.0 collective-permute-done.9.refs_2_
  20.4 0.0 collective-permute-done.8.refs_1_
  20.4 0.0 copy-done
  20.4 2.5 %shard_map.163 = bf16[64,9216]{1,0:T(8,128)(2,1)} custom-call(s32[64,128]{1,0:T(8,128)S(1)} %bitcast.31, bf16[8,9216]{1,0:T(8,128)(2,1)S(1)} %copy-done, bf16[8,9216]{1,0:T(8,128)(2,1)S(1)} %collective-permute-done.8.refs_1_, bf16[8,9216]{1,0:T(8,128)(2,1)S(1)} %collective-permute-done.9.refs_2_, bf16[8,9216]{1,0:T(8,128)(2,1)S(1)} %collective-permute-done.10.refs_3_), custom_call_target="tpu_custom_call" | custom-call | flops 40000000 | bytes 2000000 | tf_op jit(solution)/shard_map/pallas_call | solution.py:291
  23.0 0.0 copy-done.1
  23.0 0.0 copy-done.2
  23.0 0.0 copy-done.3
  23.0 74.9 %conditional.1 = (bf16[4768,256]{1,0:T(8,128)(2,1)}, bf16[4608,256]{1,0:T(8,128)(2,1)}, f32[4768,256]{1,0:T(8,128)S(1)}, bf16[128,256]{1,0:T(8,128)(2,1)}, bf16[...) conditional(s32[]{:T(128)} %clamp.3, (bf16[4768,256]{1,0:T(8,128)(2,1)}, ...), branch_computations={%region_0.1_spmd, %region_1.2_spmd, %region_2.3_spmd, %region_3.4_... | conditional | flops 16000000000 | bytes 29303928 | solution.py:472
  23.2 5.8 %all-to-all-start.4 = ((bf16[8,8,9216]{2,1,0:T(8,128)(2,1)}), bf16[8,8,9216]{2,1,0:T(8,128)(2,1)S(1)}, u32[]{:S(2)}, u32[]{:S(2)}) async-start(bf16[8,8,9216]{2,1,0:T(8,128)(2,1)} %get-tuple-element.204), calls=%async_computation.4 | async-start | bytes 2359296 | tf_op jit(solution)/shard_map/cond/branch_4_fun/all_to_all | solution.py:453
  29.1 2.9 %collective-permute-start.4 = (bf16[4768,256]{1,0:T(8,128)(2,1)}, bf16[4768,256]{1,0:T(8,128)(2,1)}, u32[]{:S(2)}, u32[]{:S(2)}) collective-permute-start(bf16[4768,256]{1,0:T(8,128)(2,1)} %get-tuple-element.200.w_hbm), channel_id=1, source_target_pairs={{0,16},{1,17},{2,18},{3,19},{4,20},{5,21},{6,22},{7,23},{8,24},{9,... | collective-permute-start | bytes 7323656 | tf_op jit(solution)/shard_map/cond/branch_4_fun/ppermute | solution.py:445
  31.9 13.5 %all-to-all-done.4 = bf16[8,8,9216]{2,1,0:T(8,128)(2,1)S(1)} async-done(((bf16[8,8,9216]{2,1,0:T(8,128)(2,1)}), bf16[8,8,9216]{2,1,0:T(8,128)(2,1)S(1)}, u32[]{:S(2)}, u32[]{:S(2)}) %all-to-all-start.4) | async-done | bytes 1179680 | tf_op jit(solution)/shard_map/cond/branch_4_fun/all_to_all | solution.py:453
  45.4 30.1 %branch_4_fun.1 = (bf16[4608,256]{1,0:T(8,128)(2,1)}, f32[4768,256]{1,0:T(8,128)S(1)}, bf16[128,256]{1,0:T(8,128)(2,1)}, bf16[16,256]{1,0:T(8,128)(2,1)}, bf16[3,256]{1,0:T(4,128)(2,1)}) custom-call(s32[1]{0:T(128)} %get-tuple-element.201.count_ref, f32[1]{0:T(128)} %get-tuple-element.202.scale_ref, bf16[32,64]{1,0:T(8,128)(2,1)S(1)} %get-tuple-element.203.sel_ref, ...), custom_call_target="tpu_custom_call" | custom-call | flops 16000000000 | bytes 16000000 | tf_op jit(solution)/shard_map/cond/branch_4_fun/pallas_call | solution.py:199
  75.5 22.4 %collective-permute-done.4 = bf16[4768,256]{1,0:T(8,128)(2,1)} collective-permute-done((bf16[4768,256]{1,0:T(8,128)(2,1)}, bf16[4768,256]{1,0:T(8,128)(2,1)}, u32[]{:S(2)}, u32[]{:S(2)}) %collective-permute-start.4) | collective-permute-done | bytes 2441248 | tf_op jit(solution)/shard_map/cond/branch_4_fun/ppermute | solution.py:445
  97.9 4.4 %shard_map.164 = (f32[4608,256]{1,0:T(8,128)}, f32[128,256]{1,0:T(8,128)}, f32[16,256]{1,0:T(8,128)}, f32[3,1,256]{2,1,0:T(1,128)}) custom-call(bf16[4768,256]{1,0:T(8,128)(2,1)} %get-tuple-element.280.t_hbm, f32[4768,256]{1,0:T(8,128)S(1)} %get-tuple-element.281.base_hbm), custom_call_target="tpu_custom_call" | custom-call | flops 1000000 | bytes 12000000 | tf_op jit(solution)/shard_map/pallas_call | solution.py:427
Async XLA Ops:
  3.4 16.1 %collective-permute-start.10 = (bf16[8,9216]{1,0:T(8,128)(2,1)}, bf16[8,9216]{1,0:T(8,128)(2,1)S(1)}, u32[]{:S(2)}, u32[]{:S(2)}) collective-permute-start(bf16[8,9216]{1,0:T(8,128)(2,1)} %get-tuple-element.278.refs_0_), channel_id=1, source_target_pairs={{0,6},{1,7},{2,4},{3,5},{4,2},{5,3},{6,0},{7,1},{8,14},{9,15},{10,... | collective-permute-start | bytes 442376 | tf_op jit(solution)/shard_map/ppermute | solution.py:449
  8.7 11.8 %collective-permute-start.9 = (bf16[8,9216]{1,0:T(8,128)(2,1)}, bf16[8,9216]{1,0:T(8,128)(2,1)S(1)}, u32[]{:S(2)}, u32[]{:S(2)}) collective-permute-start(bf16[8,9216]{1,0:T(8,128)(2,1)} %get-tuple-element.278.refs_0_), channel_id=1, source_target_pairs={{0,4},{1,5},{2,6},{3,7},{4,0},{5,1},{6,2},{7,3},{8,12},{9,13},{10,... | collective-permute-start | bytes 442376 | tf_op jit(solution)/shard_map/ppermute | solution.py:449
  8.7 11.8 %collective-permute-start.8 = (bf16[8,9216]{1,0:T(8,128)(2,1)}, bf16[8,9216]{1,0:T(8,128)(2,1)S(1)}, u32[]{:S(2)}, u32[]{:S(2)}) collective-permute-start(bf16[8,9216]{1,0:T(8,128)(2,1)} %get-tuple-element.278.refs_0_), channel_id=1, source_target_pairs={{0,2},{1,3},{2,0},{3,1},{4,6},{5,7},{6,4},{7,5},{8,10},{9,11},{10,... | collective-permute-start | bytes 442376 | tf_op jit(solution)/shard_map/ppermute | solution.py:449
  9.0 10.4 %all-to-all-start.8 = ((s32[8,8,128]{2,1,0:T(8,128)}), s32[8,8,128]{2,1,0:T(8,128)S(1)}, u32[]{:S(2)}, u32[]{:S(2)}) async-start(s32[8,8,128]{2,1,0:T(8,128)} %get-tuple-element.277), calls=%async_computation.8 | async-start | bytes 65536 | tf_op jit(solution)/shard_map/all_to_all | solution.py:453
  15.5 5.0 %copy-start = (bf16[8,9216]{1,0:T(8,128)(2,1)S(1)}, bf16[8,9216]{1,0:T(8,128)(2,1)}, u32[]{:S(2)}) copy-start(bf16[8,9216]{1,0:T(8,128)(2,1)} %get-tuple-element.278.refs_0_) | copy-start | bytes 442372
  15.5 7.5 %copy-start.1 = (f32[1,128,256]{2,1,0:T(8,128)S(1)}, f32[1,128,256]{2,1,0:T(8,128)}, u32[]{:S(2)}) copy-start(f32[1,128,256]{2,1,0:T(8,128)} %param.24) | copy-start | bytes 393220
  15.5 7.5 %copy-start.2 = (f32[1,16,256]{2,1,0:T(8,128)S(1)}, f32[1,16,256]{2,1,0:T(8,128)}, u32[]{:S(2)}) copy-start(f32[1,16,256]{2,1,0:T(8,128)} %param.26) | copy-start | bytes 49156
  15.5 7.5 %copy-start.3 = (f32[1,3,256]{2,0,1:T(1,128)S(1)}, f32[1,3,256]{2,0,1:T(1,128)}, u32[]{:S(2)}) copy-start(f32[1,3,256]{2,0,1:T(1,128)} %param.27) | copy-start | bytes 9220
  23.2 22.2 %all-to-all-start.4 = ((bf16[8,8,9216]{2,1,0:T(8,128)(2,1)}), bf16[8,8,9216]{2,1,0:T(8,128)(2,1)S(1)}, u32[]{:S(2)}, u32[]{:S(2)}) async-start(bf16[8,8,9216]{2,1,0:T(8,128)(2,1)} %get-tuple-element.204), calls=%async_computation.4 | async-start | bytes 2359296 | tf_op jit(solution)/shard_map/cond/branch_4_fun/all_to_all | solution.py:453
  29.1 68.8 %collective-permute-start.4 = (bf16[4768,256]{1,0:T(8,128)(2,1)}, bf16[4768,256]{1,0:T(8,128)(2,1)}, u32[]{:S(2)}, u32[]{:S(2)}) collective-permute-start(bf16[4768,256]{1,0:T(8,128)(2,1)} %get-tuple-element.200.w_hbm), channel_id=1, source_target_pairs={{0,16},{1,17},{2,18},{3,19},{4,20},{5,21},{6,22},{7,23},{8,24},{9,... | collective-permute-start | bytes 7323656 | tf_op jit(solution)/shard_map/cond/branch_4_fun/ppermute | solution.py:445

commit v2 on v1

--- a/solution.py
+++ b/solution.py
@@ -26,17 +26,16 @@
 
 
 def main_kernel(
-    count_ref, scale_ref, sel_ref, got_ref, w_hbm, bias_ref, conv_hbm, stem_ref, head_ref,
+    weight_ref, sel_ref, got_ref, w_hbm, bias_ref, conv_hbm, stem_ref, head_ref,
     gconv_hbm, base_hbm, gstem_ref, ghead_ref, gbias_ref,
-    wb, mine, gb, x_s, heat_s, act, act_t, grad, whe, err_s, err_t, bsum, gstem_acc,
-    tail, wsem, msem, tsem, osem, gsem, *, U, UB):
+    wb, mine, gb, x_t, heat_s, act, act_t, grad, whe, err_s, err_t, bsum,
+    tail, wsem, msem, tsem, osem, gsem, *, U, UB, HU, HV, ONE):
     wcopies = []
     for k, (lo, n) in enumerate(((ROW_STEM, PACKED - ROW_STEM), (0, ROW_STEM))):
         c = pltpu.make_async_copy(w_hbm.at[pl.ds(lo, n)], wb.at[pl.ds(lo, n)], wsem.at[k])
         c.start()
         wcopies.append(c)
     load_mine = pltpu.make_async_copy(conv_hbm, mine, msem)
-    load_mine.start()
 
     edge = jnp.zeros((32, 256), bf16)
 
@@ -64,13 +63,14 @@
     def _(u):
         r = dot(sel, got_ref[:, block(u, 1024)]).astype(bf16)
         x = jnp.concatenate([r[:, v * 128:(v + 1) * 128] for v in range(8)], axis=0)
-        x_s[u] = x
+        x_t[:, block(u, 256)] = x.T
         heat_s[block(u, 32), :] = dot(sel, got_ref[:, pl.ds(pl.multiple_of(8192 + u * 128, 128), 128)])
         pre = dot(x, ws) + b0
         a = jnp.maximum(pre, 0.0).astype(bf16)
         act[0, u + 1, 32:288, :] = a
 
     wcopies[1].wait()
+    load_mine.start()
     n = 8 // U
 
     @pl.loop(0, 2 * n)
@@ -92,8 +92,6 @@
             a = jnp.maximum(p, 0.0).astype(bf16)
             act[s + 1, u + e + 1, 32:288, :] = a
 
-    count = count_ref[0]
-    scale = scale_ref[0]
     wh = wb[ROW_HEAD:ROW_HEAD + 16, :]
 
     def predict(v, pred):
@@ -102,9 +100,8 @@
         a = act[2, 1:9, pl.ds(pl.multiple_of(v * 32 + 32, 32), 32), :].reshape(256, 256)
         return pred + lax.dot_general(a, whe[v], NT, preferred_element_type=f32)
 
-    pred = lax.fori_loop(0, 8, predict, jnp.zeros((256, 128), f32))
-    row = lax.broadcasted_iota(jnp.int32, (256, 128), 0)
-    err = jnp.where((row & 31) < count, (pred - heat_s[...]) * scale, 0.0).astype(bf16)
+    pred = lax.fori_loop(0, 8, predict, jnp.zeros((256, 128), f32), unroll=HU)
+    err = ((pred - heat_s[...]) * jnp.concatenate([weight_ref[...]] * 8, axis=0)).astype(bf16)
     err_s[...] = err
     err_t[...] = err.T
     bsum[...] = jnp.zeros_like(bsum)
@@ -117,7 +114,7 @@
         grad[2, 1:9, at, :] = d.reshape(8, 32, 256)
         return gh + dot(err_t[block(v, 16), :], a)
 
-    gh = lax.fori_loop(0, 8, spread, jnp.zeros((16, 256), f32))
+    gh = lax.fori_loop(0, 8, spread, jnp.zeros((16, 256), f32), unroll=HV)
     ghead_ref[...] = gh.astype(bf16)
     tail[128:144, :] = 0.5 * head_ref[...] - 0.1 * gh
 
@@ -128,15 +125,24 @@
         q = k // m
         s = 1 - q
         u = (k - q * m) * UB
-        da = None
-        for i in range(3):
-            for j in range(3):
-                ii, jj = 2 - i, 2 - j
-                rows = [grad[s + 1, u + e + ii, jj * 32:jj * 32 + 256, :] for e in range(UB)]
-                lhs = rows[0] if UB == 1 else jnp.concatenate(rows, axis=0)
-                w = wb[pl.ds(pl.multiple_of(s * 2304 + (3 * i + j) * 256, 256), 256), :]
-                t = lax.dot_general(lhs, w, NT, preferred_element_type=f32)
-                da = t if da is None else da + t
+        if ONE:
+            order = [(i, j) for i in range(3) for j in range(3)]
+            rows = [jnp.concatenate([grad[s + 1, u + e + 2 - i, (2 - j) * 32:(2 - j) * 32 + 256, :] for i, j in order], axis=1)
+                    for e in range(UB)]
+            lhs = rows[0] if UB == 1 else jnp.concatenate(rows, axis=0)
+            w = jnp.concatenate(
+                [wb[pl.ds(pl.multiple_of(s * 2304 + (3 * i + j) * 256, 256), 256), :] for i, j in order], axis=1)
+            da = lax.dot_general(lhs, w, NT, preferred_element_type=f32)
+        else:
+            da = None
+            for i in range(3):
+                for j in range(3):
+                    ii, jj = 2 - i, 2 - j
+                    rows = [grad[s + 1, u + e + ii, jj * 32:jj * 32 + 256, :] for e in range(UB)]
+                    lhs = rows[0] if UB == 1 else jnp.concatenate(rows, axis=0)
+                    w = wb[pl.ds(pl.multiple_of(s * 2304 + (3 * i + j) * 256, 256), 256), :]
+                    t = lax.dot_general(lhs, w, NT, preferred_element_type=f32)
+                    da = t if da is None else da + t
         keep = q.astype(f32)
         for e in range(UB):
             d = da[e * 256:(e + 1) * 256] + keep * grad[2, u + e + 1, 32:288, :].astype(f32)
@@ -147,13 +153,7 @@
     gbias_ref[...] = bsum[0:3, :].astype(bf16)
     tail[144:152, :] = 0.5 * jnp.concatenate([bias_ref[0], bias_ref[1], bias_ref[2], jnp.zeros((5, 256), f32)], axis=0) - 0.1 * bsum[...]
     tail[152:160, :] = jnp.zeros((8, 256), f32)
-    gstem_acc[...] = jnp.zeros_like(gstem_acc)
-
-    @pl.loop(0, 8)
-    def _(u):
-        gstem_acc[...] += lax.dot_general(x_s[u], grad[0, u + 1, 32:288, :], TN, preferred_element_type=f32)
-
-    gs = gstem_acc[...]
+    gs = dot(x_t[...], grad[0, 1:9, 32:288, :].reshape(2048, 256))
     gstem_ref[...] = gs.astype(bf16)
     tail[0:128, :] = 0.5 * stem_ref[...] - 0.1 * gs
     save_tail = pltpu.make_async_copy(tail, base_hbm.at[pl.ds(ROW_STEM, 160)], tsem)
@@ -190,51 +190,60 @@
     save_tail.wait()
 
 
-def main_call(count, scale, sel, got, packed, bias, conv, stem, head, U=4, UB=2):
+def main_call(weight, sel, got, packed, bias, conv, stem, head, U=2, UB=2, HU=8, HV=2, ONE=False):
     vm = pl.BlockSpec(memory_space=pltpu.VMEM)
-    sm = pl.BlockSpec(memory_space=pltpu.SMEM)
     hb = pl.BlockSpec(memory_space=pltpu.HBM)
     S = jax.ShapeDtypeStruct
     maps = pltpu.VMEM((3, 10, 320, 256), bf16)
     return pl.pallas_call(
-        functools.partial(main_kernel, U=U, UB=UB),
+        functools.partial(main_kernel, U=U, UB=UB, HU=HU, HV=HV, ONE=ONE),
         out_shape=(S((4608, 256), bf16), S((PACKED, 256), f32), S((128, 256), bf16), S((16, 256), bf16), S((3, 256), bf16)),
-        in_specs=[sm, sm, vm, vm, hb, vm, hb, vm, vm],
+        in_specs=[vm, vm, vm, hb, vm, hb, vm, vm],
         out_specs=(hb, hb, vm, vm, vm),
         scratch_shapes=[
             pltpu.VMEM((PACKED, 256), bf16), pltpu.VMEM((4608, 256), f32), pltpu.VMEM((4608, 256), bf16),
-            pltpu.VMEM((8, 256, 128), bf16), pltpu.VMEM((256, 128), f32), maps, pltpu.VMEM((2, 3, 256, 2560), bf16), maps,
+            pltpu.VMEM((128, 2048), bf16), pltpu.VMEM((256, 128), f32), maps, pltpu.VMEM((2, 3, 256, 2560), bf16), maps,
             pltpu.VMEM((8, 128, 256), bf16), pltpu.VMEM((256, 128), bf16), pltpu.VMEM((128, 256), bf16),
-            pltpu.VMEM((8, 256), f32), pltpu.VMEM((128, 256), f32), pltpu.VMEM((160, 256), f32),
+            pltpu.VMEM((8, 256), f32), pltpu.VMEM((160, 256), f32),
             pltpu.SemaphoreType.DMA((2,)), pltpu.SemaphoreType.DMA, pltpu.SemaphoreType.DMA, pltpu.SemaphoreType.DMA((18,)), pltpu.SemaphoreType.DMA((18,)),
         ],
         compiler_params=pltpu.CompilerParams(vmem_limit_bytes=48 * 1024 * 1024),
         cost_estimate=pl.CostEstimate(flops=16_000_000_000, bytes_accessed=16_000_000, transcendentals=0),
-    )(count, scale, sel, got, packed, bias, conv, stem, head)
+    )(weight, sel, got, packed, bias, conv, stem, head)
 
 
 BOTH = ("grp", "dev")
-COLUMNS = [[y * 8 + z * 2 + c for y in range(4) for c in range(2)] for z in range(4)]
-
-
-def prep_kernel(count_ref, zpos_ref, req_hbm, home_hbm, maps_hbm, heat_hbm, asked_ref, sel_ref, mine_ref, req, home, heat, maps, wide, sems):
+SAME_Z = [[y * 8 + z * 2 + c for y in range(4) for c in range(2)] for z in range(4)]
+SAME_Y = [[y * 8 + z * 2 + c for z in range(4) for c in range(2)] for y in range(4)]
+Y_BITS = (3, 4)
+
+
+def prep_kernel(me_ref, step_ref, count_ref, req_hbm, home_hbm, maps_hbm, heat_hbm, asked_ref, sel_ref, weight_ref, mine_ref,
+                req, home, heat, maps, wide, sems):
     copies = [
         pltpu.make_async_copy(src, dst, sems.at[k])
-        for k, (src, dst) in enumerate(((maps_hbm, maps), (heat_hbm, heat), (req_hbm, req), (home_hbm, home)))
+        for k, (src, dst) in enumerate((
+            (maps_hbm, maps), (heat_hbm, heat), (req_hbm, req), (home_hbm, home),
+        ))
     ]
     for c in copies:
         c.start()
+    for c in copies[2:]:
+        c.wait()
     count = count_ref[0]
-    copies[2].wait()
-    copies[3].wait()
+    bit = step_ref[0] & 7
+    on_y = ((bit == Y_BITS[0]) | (bit == Y_BITS[1])).astype(jnp.int32)
     i = lax.broadcasted_iota(jnp.int32, (32, 32), 0)
     j = lax.broadcasted_iota(jnp.int32, (32, 32), 1)
     wanted = jnp.sum(jnp.where(i == j, req[...], 0), axis=1, keepdims=True)
     lane = lax.broadcasted_iota(jnp.int32, (32, 256), 1)
     pos = jnp.sum(jnp.where(lane == wanted, home[...], 0), axis=1, keepdims=True)
     owner = pos >> 3
-    column = (owner >> 3) * 2 + (owner & 1)
-    row = (((owner >> 1) & 3) ^ zpos_ref[0]) * 8 + (pos & 7)
+    along = 1 + 2 * on_y
+    other = 4 - along
+    here = (me_ref[0] >> along) & 3
+    column = ((owner >> other) & 3) * 2 + (owner & 1)
+    row = (((owner >> along) & 3) ^ here) * 8 + (pos & 7)
     across_lanes = jnp.sum(jnp.where(i == j, column, 0), axis=0, keepdims=True)
     live = lax.broadcasted_iota(jnp.int32, (32, 1), 0) < count
     earlier = (across_lanes == column) & (j < i) & (j < count)
@@ -242,6 +251,8 @@
     lane64 = lax.broadcasted_iota(jnp.int32, (32, 64), 1)
     pick = jnp.where((lane64 == column * 8 + rank) & live, 1.0, 0.0)
     sel_ref[...] = pick.astype(bf16)
+    total = jnp.full((32, 128), count * 1024, jnp.int32).astype(f32)
+    weight_ref[...] = jnp.where(lax.broadcasted_iota(jnp.int32, (32, 128), 0) < count, 2.0 / total, 0.0)
     value = jnp.broadcast_to((row + 1).astype(f32), (32, 128)).astype(bf16)
     asked = lax.dot_general(pick.astype(bf16), value, TN, preferred_element_type=f32)
     asked_ref[...] = (asked.astype(jnp.int32) - 1).reshape(8, 8, 128)
@@ -253,16 +264,16 @@
     mine_ref[:, 8192:9216] = heat[...]
 
 
-def prep(count, zpos, req, home, maps, heat):
+def prep(me, number, count, req, home, maps, heat):
     vm = pl.BlockSpec(memory_space=pltpu.VMEM)
     sm = pl.BlockSpec(memory_space=pltpu.SMEM)
     hb = pl.BlockSpec(memory_space=pltpu.HBM)
     S = jax.ShapeDtypeStruct
     return pl.pallas_call(
         prep_kernel,
-        out_shape=(S((8, 8, 128), jnp.int32), S((32, 64), bf16), S((8, 9216), bf16)),
-        in_specs=[sm, sm, hb, hb, hb, hb],
-        out_specs=(vm, vm, vm),
+        out_shape=(S((8, 8, 128), jnp.int32), S((32, 64), bf16), S((32, 128), f32), S((8, 9216), bf16)),
+        in_specs=[sm, sm, sm, hb, hb, hb, hb],
+        out_specs=(vm, vm, vm, vm),
         scratch_shapes=[
             pltpu.VMEM((1, 32), jnp.int32),
             pltpu.VMEM((1, 256), jnp.int32),
@@ -272,7 +283,7 @@
             pltpu.SemaphoreType.DMA((4,)),
         ],
         compiler_params=pltpu.CompilerParams(vmem_limit_bytes=60 * 1024 * 1024),
-    )(count, zpos, req, home, maps, heat)
+    )(me, number, count, req, home, maps, heat)
 
 
 def choose_kernel(table_ref, *refs):
@@ -445,33 +456,39 @@
     return lax.ppermute(array, BOTH, [(i, i ^ (1 << bit)) for i in range(256)])
 
 
-def along_z(array, mask):
-    return lax.ppermute(array, "dev", [(i, i ^ (mask << 1)) for i in range(32)])
-
-
-def among(array):
-    return lax.all_to_all(array, "dev", split_axis=0, concat_axis=0, axis_index_groups=COLUMNS, tiled=True)
-
-
-def step(bit, counts, scale, sel, send, packed, bias, conv, stem, head):
+def among(array, groups):
+    return lax.all_to_all(array, "dev", split_axis=0, concat_axis=0, axis_index_groups=groups, tiled=True)
+
+
+def gather(on_y, asked, mine, conv, stem, head, bias):
+    shift, groups = (3, SAME_Y) if on_y else (1, SAME_Z)
+    others = [lax.ppermute(mine, "dev", [(i, i ^ (m << shift)) for i in range(32)]) for m in (1, 2, 3)]
+    table = among(asked, groups)
+    packed = pack(conv, stem, head, bias)
+    send = choose(table.reshape(64, 128), mine, *others)
+    return packed, send
+
+
+def step(bit, weight, sel, send, packed, bias, conv, stem, head):
     theirs = swap(packed, bit)
-    got = among(send)
-    outs = main_call(counts, scale, sel, got.reshape(64, 9216), packed, bias, conv, stem, head)
+    got = among(send, SAME_Y if bit in Y_BITS else SAME_Z)
+    outs = main_call(weight, sel, got.reshape(64, 9216), packed, bias, conv, stem, head)
     return (theirs, *outs)
 
 
 def local(step_number, maps, heat, home, requests, counts, stem, conv, head, bias):
     stem, conv, head, bias = stem[0], conv.reshape(4608, 256), head[0], jnp.transpose(bias, (1, 0, 2))
-    zpos = ((lax.axis_index("dev") >> 1) & 3).astype(jnp.int32).reshape(1)
-    scale = 2.0 / (counts.astype(f32) * 1024.0)
-    asked, sel, mine = prep(counts, zpos, requests, home, maps, heat)
-    others = [along_z(mine, mask) for mask in (1, 2, 3)]
-    table = among(asked)
-    packed = pack(conv, stem, head, bias)
-    send = choose(table.reshape(64, 128), mine, *others)
+    bit = step_number & 7
+    on_y = ((bit == Y_BITS[0]) | (bit == Y_BITS[1])).astype(jnp.int32)
+    me = lax.axis_index("dev").astype(jnp.int32)
+    asked, sel, weight, mine = prep(me.reshape(1), step_number.reshape(1), counts, requests, home, maps, heat)
+    packed, send = lax.switch(
+        on_y, [functools.partial(gather, 0), functools.partial(gather, 1)],
+        asked, mine, conv, stem, head, bias,
+    )
     outs = lax.switch(
-        step_number % 8, [functools.partial(step, b) for b in range(8)],
-        counts, scale, sel, send.reshape(8, 8, 9216), packed, bias, conv, stem, head,
+        bit, [functools.partial(step, b) for b in range(8)],
+        weight, sel, send.reshape(8, 8, 9216), packed, bias, conv, stem, head,
     )
     theirs, gconv, base, gstem, ghead, gbias = outs
     new, nstem, nhead, nbias = mix(theirs, base)

time: 103 us -> 88.9 us (0.86)
  waiting for transfers between devices: 37.1 us -> 27 us
  Pallas kernels: 42.7 us -> 40.4 us
  starting transfers between devices: 20 us -> 18.7 us
    ppermute x1, waiting for transfers between devices: 22.4 us -> 0.01 us  [swap(): return lax.ppermute(array, BOTH, [(i, i ^ 1 << bit) for i in range(256)])]
    all_to_all x2, waiting for transfers between devices: 13.8 us -> 27 us  [among(): lax.all_to_all(array, 'dev', split_axis=0, concat_axis=0, axis_index_grou...]
    pallas_call x1, Pallas kernels: 30.1 us -> 27.8 us  [main_call(): pl.pallas_call(functools.partial(main_kernel, U=U, UB=UB, HU=HU, HV=HV, O...]
    ppermute x3, starting transfers between devices: 5.63 us -> 4.32 us  [gather(): lax.ppermute(mine, 'dev', [(i, i ^ m << shift) for i in range(32)])]
  transfers between devices with their start and end apart: 6 -> 6, of which waited for: 4 -> 2; matrix products, arithmetic and copies ran while one was open for 0% -> 0% of each run, Pallas kernels for 33% -> 35%
where the time goes in v2:
time: 88.9 us; the launch traced here: 88.6 us
  Pallas kernels  40.4 us (45%)
  waiting for transfers between devices  27 us (30%)
  starting transfers between devices  18.7 us (21%)
  between operations  2.18 us (2%)
    pallas_call x1, Pallas kernels, main_call(): pl.pallas_call(functools.partial(main_kernel, U=U, UB=UB, HU=HU, HV=HV, O...  27.8 us
    all_to_all x2, waiting for transfers between devices, among(): lax.all_to_all(array, 'dev', split_axis=0, concat_axis=0, axis_index_grou...  27 us
    all_to_all x2, starting transfers between devices, among(): lax.all_to_all(array, 'dev', split_axis=0, concat_axis=0, axis_index_grou...  11.5 us
    pallas_call x1, Pallas kernels, mix(): pl.pallas_call(mix_kernel, out_shape=(S((4608, 256), f32), S((128, 256),...  4.4 us
    ppermute x3, starting transfers between devices, gather(): lax.ppermute(mine, 'dev', [(i, i ^ m << shift) for i in range(32)])  4.32 us
    pallas_call x1, Pallas kernels, pack(): pl.pallas_call(pack_kernel, out_shape=jax.ShapeDtypeStruct((PACKED, 256),...  3.6 us
    ppermute x1, starting transfers between devices, swap(): return lax.ppermute(array, BOTH, [(i, i ^ 1 << bit) for i in range(256)])  2.92 us
    pallas_call x1, Pallas kernels, choose(): pl.pallas_call(choose_kernel, out_shape=jax.ShapeDtypeStruct((64, 9216),...  2.5 us
  transfers between devices with their start and end apart: 6, of which 2 were waited for; matrix products, arithmetic and copies ran while one was open for 0% of the time, Pallas kernels for 35%

profile of v2, /device:TPU:1, one launch (start us, length us, event | category | flops | bytes accessed | tf_op | source)
XLA Modules:
  0.0 88.6 jit_solution(9113668199942224748)
XLA Ops:
  1.9 2.1 %shard_map.161 = (s32[8,8,128]{2,1,0:T(8,128)}, bf16[32,64]{1,0:T(8,128)(2,1)S(1)}, f32[32,128]{1,0:T(8,128)S(1)}, bf16[8,9216]{1,0:T(8,128)(2,1)S(1)}) custom-call(s32[1]{0:T(128)} %bitcast.16.me_ref, s32[1]{0:T(128)} %bitcast.26.step_ref, s32[1]{0:T(128)S(6)} %copy.71.count_ref, s32[1,32]{1,0:T(1,128)} %req_hbm.1, s32[1,256]{1,0:T(1,128)} %home_hbm.1, ...), custom_call_target="tpu_custom_call" | custom-call | tf_op jit(solution)/shard_map/pallas_call | solution.py:272
  4.0 19.1 %conditional.2 = (bf16[4768,256]{1,0:T(8,128)(2,1)}, bf16[8,8,9216]{2,1,0:T(8,128)(2,1)}) conditional(s32[]{:T(128)} %clamp.7, (f32[4608,256]{1,0:T(8,128)}, f32[128,256]{1,0:T(8,128)}, f32[16,256]{1,0:T(8,128)}, f32[3,1,256]{2,1,0:T(1,128)}, s32[8,8,128]{2,1,0:T(8,128)}, /*index=5*/bf16[8,9216]{1,0:T(8,128)(2,1)S(1)}) %tuple.93, ...), branch_computations={%region_0.0_spmd, %region_1.0_spmd} | conditional | flops 41000000 | bytes 10867944 | solution.py:485
  4.0 3.6 %collective-permute-start.5 = (bf16[8,9216]{1,0:T(8,128)(2,1)S(1)}, bf16[8,9216]{1,0:T(8,128)(2,1)S(1)}, u32[]{:S(2)}, u32[]{:S(2)}) collective-permute-start(bf16[8,9216]{1,0:T(8,128)(2,1)S(1)} %get-tuple-element.164.refs_0_), channel_id=1, source_target_pairs={{0,24},{1,25},{2,26},{3,27},{4,28},{5,29},{6,30},{7,31},{8,16},{9,... | collective-permute-start | bytes 442376 | tf_op jit(solution)/shard_map/cond/branch_1_fun/ppermute | solution.py:465
  7.7 0.3 collective-permute-start.4
  8.0 0.3 collective-permute-start.3
  8.3 7.3 %all-to-all-start.1 = ((s32[8,8,128]{2,1,0:T(8,128)}), s32[8,8,128]{2,1,0:T(8,128)S(1)}, u32[]{:S(2)}, u32[]{:S(2)}) async-start(s32[8,8,128]{2,1,0:T(8,128)} %get-tuple-element.163), calls=%async_computation.1 | async-start | bytes 65536 | tf_op jit(solution)/shard_map/cond/branch_1_fun/all_to_all | solution.py:460
  15.6 3.6 %branch_1_fun.3 = bf16[4768,256]{1,0:T(8,128)(2,1)} custom-call(f32[4608,256]{1,0:T(8,128)} %get-tuple-element.159.conv_hbm, f32[128,256]{1,0:T(8,128)} %get-tuple-element.160.stem_hbm, f32[16,256]{1,0:T(8,128)} %get-tuple-element.161.head_hbm, f32[3,1,256]{2,1,0:T(1,128)} %get-tuple-element.162.bias_hbm), custom_call_target="tpu_custom_call" | custom-call | flops 1000000 | bytes 7000000 | tf_op jit(solution)/shard_map/cond/branch_1_fun/pallas_call | solution.py:366
  19.2 1.4 %all-to-all-done.1 = s32[8,8,128]{2,1,0:T(8,128)S(1)} async-done(((s32[8,8,128]{2,1,0:T(8,128)}), s32[8,8,128]{2,1,0:T(8,128)S(1)}, u32[]{:S(2)}, u32[]{:S(2)}) %all-to-all-start.1) | async-done | bytes 32800 | tf_op jit(solution)/shard_map/cond/branch_1_fun/all_to_all | solution.py:460
  20.6 0.0 collective-permute-done.5.refs_3_
  20.6 0.0 collective-permute-done.4.refs_2_
  20.6 0.0 collective-permute-done.3.refs_1_
  20.6 2.5 %branch_1_fun.4 = bf16[64,9216]{1,0:T(8,128)(2,1)} custom-call(s32[64,128]{1,0:T(8,128)S(1)} %bitcast.36, bf16[8,9216]{1,0:T(8,128)(2,1)S(1)} %get-tuple-element.164.refs_0_, bf16[8,9216]{1,0:T(8,128)(2,1)S(1)} %collective-permute-done.3.refs_1_, bf16[8,9216]{1,0:T(8,128)(2,1)S(1)} %collective-permute-done.4.refs_2_, ...), custom_call_target="tpu_custom_call" | custom-call | flops 40000000 | bytes 2000000 | tf_op jit(solution)/shard_map/cond/branch_1_fun/pallas_call | solution.py:302
  23.1 60.9 %conditional.3 = (bf16[4768,256]{1,0:T(8,128)(2,1)}, bf16[4608,256]{1,0:T(8,128)(2,1)}, f32[4768,256]{1,0:T(8,128)S(1)}, bf16[128,256]{1,0:T(8,128)(2,1)}, bf16[...) conditional(s32[]{:T(128)} %clamp.6, (bf16[4768,256]{1,0:T(8,128)(2,1)}, ...), branch_computations={%region_2.0_spmd, %region_3.0_spmd, %region_4.0_spmd, %region_5.0_... | conditional | flops 16000000000 | bytes 29303928 | solution.py:489
  23.1 4.2 %all-to-all-start.6 = ((bf16[8,8,9216]{2,1,0:T(8,128)(2,1)}), bf16[8,8,9216]{2,1,0:T(8,128)(2,1)S(1)}, u32[]{:S(2)}, u32[]{:S(2)}) async-start(bf16[8,8,9216]{2,1,0:T(8,128)(2,1)} %get-tuple-element.220), calls=%async_computation.6 | async-start | bytes 2359296 | tf_op jit(solution)/shard_map/cond/branch_4_fun/all_to_all | solution.py:460
  27.3 2.9 %collective-permute-start.10 = (bf16[4768,256]{1,0:T(8,128)(2,1)}, bf16[4768,256]{1,0:T(8,128)(2,1)}, u32[]{:S(2)}, u32[]{:S(2)}) collective-permute-start(bf16[4768,256]{1,0:T(8,128)(2,1)} %get-tuple-element.217.w_hbm), channel_id=1, source_target_pairs={{0,16},{1,17},{2,18},{3,19},{4,20},{5,21},{6,22},{7,23},{8,24},{9,... | collective-permute-start | bytes 7323656 | tf_op jit(solution)/shard_map/cond/branch_4_fun/ppermute | solution.py:456
  30.2 25.6 %all-to-all-done.6 = bf16[8,8,9216]{2,1,0:T(8,128)(2,1)S(1)} async-done(((bf16[8,8,9216]{2,1,0:T(8,128)(2,1)}), bf16[8,8,9216]{2,1,0:T(8,128)(2,1)S(1)}, u32[]{:S(2)}, u32[]{:S(2)}) %all-to-all-start.6) | async-done | bytes 1179680 | tf_op jit(solution)/shard_map/cond/branch_4_fun/all_to_all | solution.py:460
  55.9 27.8 %branch_4_fun.1 = (bf16[4608,256]{1,0:T(8,128)(2,1)}, f32[4768,256]{1,0:T(8,128)S(1)}, bf16[128,256]{1,0:T(8,128)(2,1)}, bf16[16,256]{1,0:T(8,128)(2,1)}, bf16[3,256]{1,0:T(4,128)(2,1)}) custom-call(f32[32,128]{1,0:T(8,128)S(1)} %get-tuple-element.218.weight_ref, bf16[32,64]{1,0:T(8,128)(2,1)S(1)} %get-tuple-element.219.sel_ref, ...), custom_call_target="tpu_custom_call" | custom-call | flops 16000000000 | bytes 16000000 | tf_op jit(solution)/shard_map/cond/branch_4_fun/pallas_call | solution.py:198
  83.7 0.0 collective-permute-done.10
  84.0 4.4 %shard_map.162 = (f32[4608,256]{1,0:T(8,128)}, f32[128,256]{1,0:T(8,128)}, f32[16,256]{1,0:T(8,128)}, f32[3,1,256]{2,1,0:T(1,128)}) custom-call(bf16[4768,256]{1,0:T(8,128)(2,1)} %get-tuple-element.299.t_hbm, f32[4768,256]{1,0:T(8,128)S(1)} %get-tuple-element.300.base_hbm), custom_call_target="tpu_custom_call" | custom-call | flops 1000000 | bytes 12000000 | tf_op jit(solution)/shard_map/pallas_call | solution.py:438
Async XLA Ops:
  4.0 16.5 %collective-permute-start.5 = (bf16[8,9216]{1,0:T(8,128)(2,1)S(1)}, bf16[8,9216]{1,0:T(8,128)(2,1)S(1)}, u32[]{:S(2)}, u32[]{:S(2)}) collective-permute-start(bf16[8,9216]{1,0:T(8,128)(2,1)S(1)} %get-tuple-element.164.refs_0_), channel_id=1, source_target_pairs={{0,24},{1,25},{2,26},{3,27},{4,28},{5,29},{6,30},{7,31},{8,16},{9,... | collective-permute-start | bytes 442376 | tf_op jit(solution)/shard_map/cond/branch_1_fun/ppermute | solution.py:465
  7.7 12.9 %collective-permute-start.4 = (bf16[8,9216]{1,0:T(8,128)(2,1)S(1)}, bf16[8,9216]{1,0:T(8,128)(2,1)S(1)}, u32[]{:S(2)}, u32[]{:S(2)}) collective-permute-start(bf16[8,9216]{1,0:T(8,128)(2,1)S(1)} %get-tuple-element.164.refs_0_), channel_id=1, source_target_pairs={{0,16},{1,17},{2,18},{3,19},{4,20},{5,21},{6,22},{7,23},{8,24},{9,... | collective-permute-start | bytes 442376 | tf_op jit(solution)/shard_map/cond/branch_1_fun/ppermute | solution.py:465
  8.0 12.6 %collective-permute-start.3 = (bf16[8,9216]{1,0:T(8,128)(2,1)S(1)}, bf16[8,9216]{1,0:T(8,128)(2,1)S(1)}, u32[]{:S(2)}, u32[]{:S(2)}) collective-permute-start(bf16[8,9216]{1,0:T(8,128)(2,1)S(1)} %get-tuple-element.164.refs_0_), channel_id=1, source_target_pairs={{0,8},{1,9},{2,10},{3,11},{4,12},{5,13},{6,14},{7,15},{8,0},{9,1},... | collective-permute-start | bytes 442376 | tf_op jit(solution)/shard_map/cond/branch_1_fun/ppermute | solution.py:465
  8.3 12.2 %all-to-all-start.1 = ((s32[8,8,128]{2,1,0:T(8,128)}), s32[8,8,128]{2,1,0:T(8,128)S(1)}, u32[]{:S(2)}, u32[]{:S(2)}) async-start(s32[8,8,128]{2,1,0:T(8,128)} %get-tuple-element.163), calls=%async_computation.1 | async-start | bytes 65536 | tf_op jit(solution)/shard_map/cond/branch_1_fun/all_to_all | solution.py:460
  23.1 32.8 %all-to-all-start.6 = ((bf16[8,8,9216]{2,1,0:T(8,128)(2,1)}), bf16[8,8,9216]{2,1,0:T(8,128)(2,1)S(1)}, u32[]{:S(2)}, u32[]{:S(2)}) async-start(bf16[8,8,9216]{2,1,0:T(8,128)(2,1)} %get-tuple-element.220), calls=%async_computation.6 | async-start | bytes 2359296 | tf_op jit(solution)/shard_map/cond/branch_4_fun/all_to_all | solution.py:460
  27.3 56.4 %collective-permute-start.10 = (bf16[4768,256]{1,0:T(8,128)(2,1)}, bf16[4768,256]{1,0:T(8,128)(2,1)}, u32[]{:S(2)}, u32[]{:S(2)}) collective-permute-start(bf16[4768,256]{1,0:T(8,128)(2,1)} %get-tuple-element.217.w_hbm), channel_id=1, source_target_pairs={{0,16},{1,17},{2,18},{3,19},{4,20},{5,21},{6,22},{7,23},{8,24},{9,... | collective-permute-start | bytes 7323656 | tf_op jit(solution)/shard_map/cond/branch_4_fun/ppermute | solution.py:456

commit v3 on v2

--- a/solution.py
+++ b/solution.py
@@ -27,9 +27,9 @@
 
 def main_kernel(
     weight_ref, sel_ref, got_ref, w_hbm, bias_ref, conv_hbm, stem_ref, head_ref,
-    gconv_hbm, base_hbm, gstem_ref, ghead_ref, gbias_ref,
+    gconv_hbm, base_ref, gstem_ref, ghead_ref, gbias_ref,
     wb, mine, gb, x_t, heat_s, act, act_t, grad, whe, err_s, err_t, bsum,
-    tail, wsem, msem, tsem, osem, gsem, *, U, UB, HU, HV, ONE):
+    wsem, msem, gsem, *, U, UB, HU, HV, ONE):
     wcopies = []
     for k, (lo, n) in enumerate(((ROW_STEM, PACKED - ROW_STEM), (0, ROW_STEM))):
         c = pltpu.make_async_copy(w_hbm.at[pl.ds(lo, n)], wb.at[pl.ds(lo, n)], wsem.at[k])
@@ -116,7 +116,7 @@
 
     gh = lax.fori_loop(0, 8, spread, jnp.zeros((16, 256), f32), unroll=HV)
     ghead_ref[...] = gh.astype(bf16)
-    tail[128:144, :] = 0.5 * head_ref[...] - 0.1 * gh
+    base_ref[ROW_HEAD:ROW_HEAD + 16, :] = 0.5 * head_ref[...] - 0.1 * gh
 
     m = 8 // UB
 
@@ -151,20 +151,17 @@
             bsum[pl.ds(s, 1), :] += jnp.sum(d.astype(f32), axis=0, keepdims=True)
 
     gbias_ref[...] = bsum[0:3, :].astype(bf16)
-    tail[144:152, :] = 0.5 * jnp.concatenate([bias_ref[0], bias_ref[1], bias_ref[2], jnp.zeros((5, 256), f32)], axis=0) - 0.1 * bsum[...]
-    tail[152:160, :] = jnp.zeros((8, 256), f32)
+    base_ref[ROW_HEAD + 16:ROW_HEAD + 24, :] = 0.5 * jnp.concatenate([bias_ref[0], bias_ref[1], bias_ref[2], jnp.zeros((5, 256), f32)], axis=0) - 0.1 * bsum[...]
+    base_ref[ROW_HEAD + 24:PACKED, :] = jnp.zeros((8, 256), f32)
     gs = dot(x_t[...], grad[0, 1:9, 32:288, :].reshape(2048, 256))
     gstem_ref[...] = gs.astype(bf16)
-    tail[0:128, :] = 0.5 * stem_ref[...] - 0.1 * gs
-    save_tail = pltpu.make_async_copy(tail, base_hbm.at[pl.ds(ROW_STEM, 160)], tsem)
-    save_tail.start()
+    base_ref[ROW_STEM:ROW_HEAD, :] = 0.5 * stem_ref[...] - 0.1 * gs
 
     load_mine.wait()
 
     def outs(t):
         r = block(t, 256)
-        return (pltpu.make_async_copy(gb.at[r], gconv_hbm.at[r], gsem.at[t]),
-                pltpu.make_async_copy(mine.at[r], base_hbm.at[r], osem.at[t]))
+        return (pltpu.make_async_copy(gb.at[r], gconv_hbm.at[r], gsem.at[t]),)
 
     @pl.loop(0, 6)
     def _(q):
@@ -178,7 +175,7 @@
             g = all_rows[i * 256:(i + 1) * 256]
             r = block(t, 256)
             gb[r, :] = g.astype(bf16)
-            mine[r, :] = 0.5 * mine[r, :] - 0.1 * g
+            base_ref[r, :] = 0.5 * mine[r, :] - 0.1 * g
             for c in outs(t):
                 c.start()
 
@@ -187,10 +184,8 @@
         for c in outs(t):
             c.wait()
 
-    save_tail.wait()
-
-
-def main_call(weight, sel, got, packed, bias, conv, stem, head, U=2, UB=2, HU=8, HV=2, ONE=False):
+
+def main_call(weight, sel, got, packed, bias, conv, stem, head, U=2, UB=2, HU=8, HV=4, ONE=False):
     vm = pl.BlockSpec(memory_space=pltpu.VMEM)
     hb = pl.BlockSpec(memory_space=pltpu.HBM)
     S = jax.ShapeDtypeStruct
@@ -199,13 +194,13 @@
         functools.partial(main_kernel, U=U, UB=UB, HU=HU, HV=HV, ONE=ONE),
         out_shape=(S((4608, 256), bf16), S((PACKED, 256), f32), S((128, 256), bf16), S((16, 256), bf16), S((3, 256), bf16)),
         in_specs=[vm, vm, vm, hb, vm, hb, vm, vm],
-        out_specs=(hb, hb, vm, vm, vm),
+        out_specs=(hb, vm, vm, vm, vm),
         scratch_shapes=[
             pltpu.VMEM((PACKED, 256), bf16), pltpu.VMEM((4608, 256), f32), pltpu.VMEM((4608, 256), bf16),
             pltpu.VMEM((128, 2048), bf16), pltpu.VMEM((256, 128), f32), maps, pltpu.VMEM((2, 3, 256, 2560), bf16), maps,
             pltpu.VMEM((8, 128, 256), bf16), pltpu.VMEM((256, 128), bf16), pltpu.VMEM((128, 256), bf16),
-            pltpu.VMEM((8, 256), f32), pltpu.VMEM((160, 256), f32),
-            pltpu.SemaphoreType.DMA((2,)), pltpu.SemaphoreType.DMA, pltpu.SemaphoreType.DMA, pltpu.SemaphoreType.DMA((18,)), pltpu.SemaphoreType.DMA((18,)),
+            pltpu.VMEM((8, 256), f32),
+            pltpu.SemaphoreType.DMA((2,)), pltpu.SemaphoreType.DMA, pltpu.SemaphoreType.DMA((18,)),
         ],
         compiler_params=pltpu.CompilerParams(vmem_limit_bytes=48 * 1024 * 1024),
         cost_estimate=pl.CostEstimate(flops=16_000_000_000, bytes_accessed=16_000_000, transcendentals=0),
@@ -380,54 +375,38 @@
     )(conv, stem, head, bias)
 
 
-MIX = 8
-PIECE = 4608 // MIX
-
-
-def mix_kernel(t_hbm, base_hbm, new_hbm, nstem_hbm, nhead_hbm, nbias_ref, theirs, wide, asem, bsem, osem):
-    def loads(k, r):
-        return (pltpu.make_async_copy(t_hbm.at[r], theirs.at[r], asem.at[k]),
-                pltpu.make_async_copy(base_hbm.at[r], wide.at[r], bsem.at[k]))
-
-    def save(k):
-        r = block(k, PIECE)
-        return pltpu.make_async_copy(wide.at[r], new_hbm.at[r], osem.at[k])
-
-    last = loads(MIX, pl.ds(ROW_STEM, 160))
-    for c in last:
-        c.start()
-    for k in range(MIX):
-        for c in loads(k, block(k, PIECE)):
-            c.start()
+PIECES = ((0, 256), (256, 512), (768, 768), (1536, 1024), (2560, 1024), (3584, 640), (4224, 384))
+
+
+def mix_kernel(t_hbm, base_ref, new_hbm, nstem_hbm, nhead_hbm, nbias_ref, theirs, wide, asem, osem):
+    def load(k, lo, n):
+        return pltpu.make_async_copy(t_hbm.at[pl.ds(lo, n)], theirs.at[pl.ds(lo, n)], asem.at[k])
 
     def mixed(lo, n):
         @pl.loop(0, n // 32)
         def _(q):
             r = pl.ds(pl.multiple_of(lo + q * 32, 32), 32)
-            wide[r, :] = wide[r, :] + 0.5 * theirs[r, :].astype(f32)
-
-    for c in last:
-        c.wait()
+            wide[r, :] = base_ref[r, :] + 0.5 * theirs[r, :].astype(f32)
+
+    loads = [load(k, lo, n) for k, (lo, n) in enumerate(PIECES + ((ROW_STEM, 160),))]
+    for c in loads:
+        c.start()
+    saves = []
+    for k, (lo, n) in enumerate(PIECES):
+        loads[k].wait()
+        mixed(lo, n)
+        saves.append(pltpu.make_async_copy(wide.at[pl.ds(lo, n)], new_hbm.at[pl.ds(lo, n)], osem.at[k]))
+        saves[-1].start()
+    loads[-1].wait()
     mixed(ROW_STEM, 160)
-    small = (pltpu.make_async_copy(wide.at[pl.ds(ROW_STEM, 128)], nstem_hbm, osem.at[MIX]),
-             pltpu.make_async_copy(wide.at[pl.ds(ROW_HEAD, 16)], nhead_hbm, osem.at[MIX + 1]))
-    for c in small:
+    last = len(PIECES)
+    saves.append(pltpu.make_async_copy(wide.at[pl.ds(ROW_STEM, 128)], nstem_hbm, osem.at[last]))
+    saves.append(pltpu.make_async_copy(wide.at[pl.ds(ROW_HEAD, 16)], nhead_hbm, osem.at[last + 1]))
+    for c in saves[-2:]:
         c.start()
     for k in range(3):
         nbias_ref[k] = wide[ROW_HEAD + 16 + k:ROW_HEAD + 17 + k, :]
-
-    @pl.loop(0, MIX)
-    def _(k):
-        for c in loads(k, block(k, PIECE)):
-            c.wait()
-        mixed(k * PIECE, PIECE)
-        save(k).start()
-
-    @pl.loop(0, MIX)
-    def _(k):
-        save(k).wait()
-
-    for c in small:
+    for c in saves:
         c.wait()
 
 
@@ -438,16 +417,15 @@
     return pl.pallas_call(
         mix_kernel,
         out_shape=(S((4608, 256), f32), S((128, 256), f32), S((16, 256), f32), S((3, 1, 256), f32)),
-        in_specs=[hb, hb],
+        in_specs=[hb, vm],
         out_specs=(hb, hb, hb, vm),
         scratch_shapes=[
             pltpu.VMEM((PACKED, 256), bf16),
             pltpu.VMEM((PACKED, 256), f32),
-            pltpu.SemaphoreType.DMA((MIX + 1,)),
-            pltpu.SemaphoreType.DMA((MIX + 1,)),
-            pltpu.SemaphoreType.DMA((MIX + 2,)),
+            pltpu.SemaphoreType.DMA((len(PIECES) + 1,)),
+            pltpu.SemaphoreType.DMA((len(PIECES) + 2,)),
         ],
-        compiler_params=pltpu.CompilerParams(vmem_limit_bytes=16 * 1024 * 1024),
+        compiler_params=pltpu.CompilerParams(vmem_limit_bytes=24 * 1024 * 1024),
         cost_estimate=pl.CostEstimate(flops=1000000, bytes_accessed=12000000, transcendentals=0),
     )(theirs, base)
 
@@ -465,12 +443,12 @@
     others = [lax.ppermute(mine, "dev", [(i, i ^ (m << shift)) for i in range(32)]) for m in (1, 2, 3)]
     table = among(asked, groups)
     packed = pack(conv, stem, head, bias)
-    send = choose(table.reshape(64, 128), mine, *others)
-    return packed, send
-
-
-def step(bit, weight, sel, send, packed, bias, conv, stem, head):
+    return packed, table, *others
+
+
+def step(bit, weight, sel, table, mine, one, two, three, packed, bias, conv, stem, head):
     theirs = swap(packed, bit)
+    send = choose(table.reshape(64, 128), mine, one, two, three).reshape(8, 8, 9216)
     got = among(send, SAME_Y if bit in Y_BITS else SAME_Z)
     outs = main_call(weight, sel, got.reshape(64, 9216), packed, bias, conv, stem, head)
     return (theirs, *outs)
@@ -482,13 +460,13 @@
     on_y = ((bit == Y_BITS[0]) | (bit == Y_BITS[1])).astype(jnp.int32)
     me = lax.axis_index("dev").astype(jnp.int32)
     asked, sel, weight, mine = prep(me.reshape(1), step_number.reshape(1), counts, requests, home, maps, heat)
-    packed, send = lax.switch(
+    packed, table, *others = lax.switch(
         on_y, [functools.partial(gather, 0), functools.partial(gather, 1)],
         asked, mine, conv, stem, head, bias,
     )
     outs = lax.switch(
         bit, [functools.partial(step, b) for b in range(8)],
-        weight, sel, send.reshape(8, 8, 9216), packed, bias, conv, stem, head,
+        weight, sel, table, mine, *others, packed, bias, conv, stem, head,
     )
     theirs, gconv, base, gstem, ghead, gbias = outs
     new, nstem, nhead, nbias = mix(theirs, base)

time: 88.9 us -> 89.6 us (level)
  waiting for transfers between devices: 27 us -> 29.3 us
  Pallas kernels: 40.4 us -> 38.8 us
    pallas_call x1, Pallas kernels: 27.8 us -> 25.4 us  [main_call(): pl.pallas_call(functools.partial(main_kernel, U=U, UB=UB, HU=HU, HV=HV, O...]
    ppermute x1, waiting for transfers between devices: 0.01 us -> 2.2 us  [swap(): return lax.ppermute(array, BOTH, [(i, i ^ 1 << bit) for i in range(256)])]
    pallas_call x1, Pallas kernels: 2.5 us -> 3.61 us  [choose(): pl.pallas_call(choose_kernel, out_shape=jax.ShapeDtypeStruct((64, 9216),...]
  transfers between devices with their start and end apart: 6 -> 6, of which waited for: 2 -> 3; matrix products, arithmetic and copies ran while one was open for 0% -> 0% of each run, Pallas kernels for 35% -> 33%
where the time goes in v3:
time: 89.6 us; the launch traced here: 89.3 us
  Pallas kernels  38.8 us (43%)
  waiting for transfers between devices  29.3 us (33%)
  starting transfers between devices  18.7 us (21%)
  between operations  2.17 us (2%)
    all_to_all x2, waiting for transfers between devices, among(): lax.all_to_all(array, 'dev', split_axis=0, concat_axis=0, axis_index_grou...  27.1 us
    pallas_call x1, Pallas kernels, main_call(): pl.pallas_call(functools.partial(main_kernel, U=U, UB=UB, HU=HU, HV=HV, O...  25.4 us
    all_to_all x2, starting transfers between devices, among(): lax.all_to_all(array, 'dev', split_axis=0, concat_axis=0, axis_index_grou...  11.5 us
    ppermute x3, starting transfers between devices, gather(): lax.ppermute(mine, 'dev', [(i, i ^ m << shift) for i in range(32)])  4.32 us
    pallas_call x1, Pallas kernels, mix(): pl.pallas_call(mix_kernel, out_shape=(S((4608, 256), f32), S((128, 256),...  4.06 us
    pallas_call x1, Pallas kernels, choose(): pl.pallas_call(choose_kernel, out_shape=jax.ShapeDtypeStruct((64, 9216),...  3.61 us
    pallas_call x1, Pallas kernels, pack(): pl.pallas_call(pack_kernel, out_shape=jax.ShapeDtypeStruct((PACKED, 256),...  3.6 us
    ppermute x1, starting transfers between devices, swap(): return lax.ppermute(array, BOTH, [(i, i ^ 1 << bit) for i in range(256)])  2.91 us
  transfers between devices with their start and end apart: 6, of which 3 were waited for; matrix products, arithmetic and copies ran while one was open for 0% of the time, Pallas kernels for 33%

profile of v3, /device:TPU:1, one launch (start us, length us, event | category | flops | bytes accessed | tf_op | source)
XLA Modules:
  0.0 89.3 jit_solution(1290382274050638057)
XLA Ops:
  1.9 2.1 %shard_map.161 = (s32[8,8,128]{2,1,0:T(8,128)}, bf16[32,64]{1,0:T(8,128)(2,1)S(1)}, f32[32,128]{1,0:T(8,128)S(1)}, bf16[8,9216]{1,0:T(8,128)(2,1)S(1)}) custom-call(s32[1]{0:T(128)} %bitcast.28.me_ref, s32[1]{0:T(128)} %bitcast.38.step_ref, s32[1]{0:T(128)S(6)} %copy.77.count_ref, s32[1,32]{1,0:T(1,128)} %req_hbm.1, s32[1,256]{1,0:T(1,128)} %home_hbm.1, ...), custom_call_target="tpu_custom_call" | custom-call | tf_op jit(solution)/shard_map/pallas_call | solution.py:267
  4.0 16.7 %conditional.2 = (bf16[4768,256]{1,0:T(8,128)(2,1)}, s32[8,8,128]{2,1,0:T(8,128)}, bf16[8,9216]{1,0:T(8,128)(2,1)}, bf16[8,9216]{1,0:T(8,128)(2,1)}, bf16[8,9216]{1,0:T(8,128)(2,1)}) conditional(s32[]{:T(128)} %clamp.7, (f32[4608,256]{1,0:T(8,128)}, f32[128,256]{1,0:T(8,128)}, f32[16,256]{1,0:T(8,128)}, f32[3,1,256]{2,1,0:T(1,128)}, ...), branch_computations={%region_0.0_spmd, %region_1.0_spmd} | conditional | flops 1000000 | bytes 8867968 | solution.py:463
  4.0 3.6 %collective-permute-start.5 = (bf16[8,9216]{1,0:T(8,128)(2,1)S(1)}, bf16[8,9216]{1,0:T(8,128)(2,1)}, u32[]{:S(2)}, u32[]{:S(2)}) collective-permute-start(bf16[8,9216]{1,0:T(8,128)(2,1)S(1)} %get-tuple-element.227), channel_id=1, source_target_pairs={{0,24},{1,25},{2,26},{3,27},{4,28},{5,29},{6,30},{7,31},{8,16},{9,... | collective-permute-start | bytes 442376 | tf_op jit(solution)/shard_map/cond/branch_1_fun/ppermute | solution.py:443
  7.7 0.3 collective-permute-start.4
  8.0 0.3 collective-permute-start.3
  8.3 7.3 %all-to-all-start.1 = ((s32[8,8,128]{2,1,0:T(8,128)}), s32[8,8,128]{2,1,0:T(8,128)}, u32[]{:S(2)}, u32[]{:S(2)}) async-start(s32[8,8,128]{2,1,0:T(8,128)} %get-tuple-element.226), calls=%async_computation.1 | async-start | bytes 65536 | tf_op jit(solution)/shard_map/cond/branch_1_fun/all_to_all | solution.py:438
  15.6 3.6 %branch_1_fun.3 = bf16[4768,256]{1,0:T(8,128)(2,1)} custom-call(f32[4608,256]{1,0:T(8,128)} %get-tuple-element.222.conv_hbm, f32[128,256]{1,0:T(8,128)} %get-tuple-element.223.stem_hbm, f32[16,256]{1,0:T(8,128)} %get-tuple-element.224.head_hbm, f32[3,1,256]{2,1,0:T(1,128)} %get-tuple-element.225.bias_hbm), custom_call_target="tpu_custom_call" | custom-call | flops 1000000 | bytes 7000000 | tf_op jit(solution)/shard_map/cond/branch_1_fun/pallas_call | solution.py:361
  19.2 1.5 %all-to-all-done.1 = s32[8,8,128]{2,1,0:T(8,128)} async-done(((s32[8,8,128]{2,1,0:T(8,128)}), s32[8,8,128]{2,1,0:T(8,128)}, u32[]{:S(2)}, u32[]{:S(2)}) %all-to-all-start.1) | async-done | bytes 32800 | tf_op jit(solution)/shard_map/cond/branch_1_fun/all_to_all | solution.py:438
  20.7 0.0 collective-permute-done.5
  20.7 0.0 collective-permute-done.4
  20.7 0.0 collective-permute-done.3
  20.7 64.3 %conditional.3 = (bf16[4768,256]{1,0:T(8,128)(2,1)}, bf16[4608,256]{1,0:T(8,128)(2,1)}, f32[4768,256]{1,0:T(8,128)S(1)}, bf16[128,256]{1,0:T(8,128)(2,1)}, bf16[...) conditional(s32[]{:T(128)} %clamp.6, (bf16[4768,256]{1,0:T(8,128)(2,1)}, ...), branch_computations={%region_2.0_spmd, %region_3.0_spmd, %region_4.0_spmd, %region_5.0_... | conditional | flops 16039999488 | bytes 31906124 | solution.py:467
  20.9 0.0 copy-start.4
  20.9 0.0 copy-start.12
  21.0 0.0 copy-start.20
  21.0 3.6 %branch_4_fun.2 = bf16[64,9216]{1,0:T(8,128)(2,1)} custom-call(s32[64,128]{1,0:T(8,128)} %bitcast.12.table_ref, bf16[8,9216]{1,0:T(8,128)(2,1)S(1)} %get-tuple-element.300.refs_0_, bf16[8,9216]{1,0:T(8,128)(2,1)} %get-tuple-element.301.refs_1_, bf16[8,9216]{1,0:T(8,128)(2,1)} %get-tuple-element.302.refs_2_, bf16[8,9216]{1,0:T(8,128)(2,1)} %get-tuple-element.303.refs_3_), custom_call_target="tpu_custom_call" | custom-call | flops 40000000 | bytes 2000000 | tf_op jit(solution)/shard_map/cond/branch_4_fun/pallas_call | solution.py:297
  24.6 4.2 %all-to-all-start.6 = ((bf16[8,8,9216]{2,1,0:T(8,128)(2,1)}), bf16[8,8,9216]{2,1,0:T(8,128)(2,1)S(1)}, u32[]{:S(2)}, u32[]{:S(2)}) async-start(bf16[8,8,9216]{2,1,0:T(8,128)(2,1)} %bitcast.13), calls=%async_computation.6 | async-start | bytes 2359296 | tf_op jit(solution)/shard_map/cond/branch_4_fun/all_to_all | solution.py:438
  28.8 2.9 %collective-permute-start.10 = (bf16[4768,256]{1,0:T(8,128)(2,1)}, bf16[4768,256]{1,0:T(8,128)(2,1)}, u32[]{:S(2)}, u32[]{:S(2)}) collective-permute-start(bf16[4768,256]{1,0:T(8,128)(2,1)} %get-tuple-element.296.w_hbm), channel_id=1, source_target_pairs={{0,16},{1,17},{2,18},{3,19},{4,20},{5,21},{6,22},{7,23},{8,24},{9,... | collective-permute-start | bytes 7323656 | tf_op jit(solution)/shard_map/cond/branch_4_fun/ppermute | solution.py:434
  31.7 25.6 %all-to-all-done.6 = bf16[8,8,9216]{2,1,0:T(8,128)(2,1)S(1)} async-done(((bf16[8,8,9216]{2,1,0:T(8,128)(2,1)}), bf16[8,8,9216]{2,1,0:T(8,128)(2,1)S(1)}, u32[]{:S(2)}, u32[]{:S(2)}) %all-to-all-start.6) | async-done | bytes 1179680 | tf_op jit(solution)/shard_map/cond/branch_4_fun/all_to_all | solution.py:438
  57.4 0.0 copy-done.4
  57.4 0.0 copy-done.12
  57.4 0.0 copy-done.20
  57.4 25.4 %branch_4_fun.3 = (bf16[4608,256]{1,0:T(8,128)(2,1)}, f32[4768,256]{1,0:T(8,128)S(1)}, bf16[128,256]{1,0:T(8,128)(2,1)}, bf16[16,256]{1,0:T(8,128)(2,1)}, bf16[3,256]{1,0:T(4,128)(2,1)}) custom-call(f32[32,128]{1,0:T(8,128)S(1)} %get-tuple-element.297.weight_ref, bf16[32,64]{1,0:T(8,128)(2,1)S(1)} %get-tuple-element.298.sel_ref, ...), custom_call_target="tpu_custom_call" | custom-call | flops 16000000000 | bytes 16000000 | tf_op jit(solution)/shard_map/cond/branch_4_fun/pallas_call | solution.py:193
  82.8 2.2 %collective-permute-done.10 = bf16[4768,256]{1,0:T(8,128)(2,1)} collective-permute-done((bf16[4768,256]{1,0:T(8,128)(2,1)}, bf16[4768,256]{1,0:T(8,128)(2,1)}, u32[]{:S(2)}, u32[]{:S(2)}) %collective-permute-start.10) | collective-permute-done | bytes 2441248 | tf_op jit(solution)/shard_map/cond/branch_4_fun/ppermute | solution.py:434
  85.0 4.1 %shard_map.162 = (f32[4608,256]{1,0:T(8,128)}, f32[128,256]{1,0:T(8,128)}, f32[16,256]{1,0:T(8,128)}, f32[3,1,256]{2,1,0:T(1,128)}) custom-call(bf16[4768,256]{1,0:T(8,128)(2,1)} %get-tuple-element.400.t_hbm, f32[4768,256]{1,0:T(8,128)S(1)} %get-tuple-element.401.base_ref), custom_call_target="tpu_custom_call" | custom-call | flops 1000000 | bytes 12000000 | tf_op jit(solution)/shard_map/pallas_call | solution.py:417
Async XLA Ops:
  4.0 16.6 %collective-permute-start.5 = (bf16[8,9216]{1,0:T(8,128)(2,1)S(1)}, bf16[8,9216]{1,0:T(8,128)(2,1)}, u32[]{:S(2)}, u32[]{:S(2)}) collective-permute-start(bf16[8,9216]{1,0:T(8,128)(2,1)S(1)} %get-tuple-element.227), channel_id=1, source_target_pairs={{0,24},{1,25},{2,26},{3,27},{4,28},{5,29},{6,30},{7,31},{8,16},{9,... | collective-permute-start | bytes 442376 | tf_op jit(solution)/shard_map/cond/branch_1_fun/ppermute | solution.py:443
  7.7 13.0 %collective-permute-start.4 = (bf16[8,9216]{1,0:T(8,128)(2,1)S(1)}, bf16[8,9216]{1,0:T(8,128)(2,1)}, u32[]{:S(2)}, u32[]{:S(2)}) collective-permute-start(bf16[8,9216]{1,0:T(8,128)(2,1)S(1)} %get-tuple-element.227), channel_id=1, source_target_pairs={{0,16},{1,17},{2,18},{3,19},{4,20},{5,21},{6,22},{7,23},{8,24},{9,... | collective-permute-start | bytes 442376 | tf_op jit(solution)/shard_map/cond/branch_1_fun/ppermute | solution.py:443
  8.0 12.7 %collective-permute-start.3 = (bf16[8,9216]{1,0:T(8,128)(2,1)S(1)}, bf16[8,9216]{1,0:T(8,128)(2,1)}, u32[]{:S(2)}, u32[]{:S(2)}) collective-permute-start(bf16[8,9216]{1,0:T(8,128)(2,1)S(1)} %get-tuple-element.227), channel_id=1, source_target_pairs={{0,8},{1,9},{2,10},{3,11},{4,12},{5,13},{6,14},{7,15},{8,0},{9,1},... | collective-permute-start | bytes 442376 | tf_op jit(solution)/shard_map/cond/branch_1_fun/ppermute | solution.py:443
  8.3 12.3 %all-to-all-start.1 = ((s32[8,8,128]{2,1,0:T(8,128)}), s32[8,8,128]{2,1,0:T(8,128)}, u32[]{:S(2)}, u32[]{:S(2)}) async-start(s32[8,8,128]{2,1,0:T(8,128)} %get-tuple-element.226), calls=%async_computation.1 | async-start | bytes 65536 | tf_op jit(solution)/shard_map/cond/branch_1_fun/all_to_all | solution.py:438
  20.9 36.4 %copy-start.4 = (f32[128,256]{1,0:T(8,128)S(1)}, f32[128,256]{1,0:T(8,128)}, u32[]{:S(2)}) copy-start(f32[128,256]{1,0:T(8,128)} %get-tuple-element.306.stem_ref) | copy-start | bytes 393220 | tf_op jit(solution)/shard_map/cond
  20.9 36.4 %copy-start.12 = (f32[16,256]{1,0:T(8,128)S(1)}, f32[16,256]{1,0:T(8,128)}, u32[]{:S(2)}) copy-start(f32[16,256]{1,0:T(8,128)} %get-tuple-element.307.head_ref) | copy-start | bytes 49156 | tf_op jit(solution)/shard_map/cond
  21.0 36.4 %copy-start.20 = (f32[3,1,256]{2,1,0:T(1,128)S(1)}, f32[3,1,256]{2,1,0:T(1,128)}, u32[]{:S(2)}) copy-start(f32[3,1,256]{2,1,0:T(1,128)} %get-tuple-element.304.bias_ref) | copy-start | bytes 9220 | tf_op jit(solution)/shard_map/cond
  24.6 32.8 %all-to-all-start.6 = ((bf16[8,8,9216]{2,1,0:T(8,128)(2,1)}), bf16[8,8,9216]{2,1,0:T(8,128)(2,1)S(1)}, u32[]{:S(2)}, u32[]{:S(2)}) async-start(bf16[8,8,9216]{2,1,0:T(8,128)(2,1)} %bitcast.13), calls=%async_computation.6 | async-start | bytes 2359296 | tf_op jit(solution)/shard_map/cond/branch_4_fun/all_to_all | solution.py:438
  28.8 56.2 %collective-permute-start.10 = (bf16[4768,256]{1,0:T(8,128)(2,1)}, bf16[4768,256]{1,0:T(8,128)(2,1)}, u32[]{:S(2)}, u32[]{:S(2)}) collective-permute-start(bf16[4768,256]{1,0:T(8,128)(2,1)} %get-tuple-element.296.w_hbm), channel_id=1, source_target_pairs={{0,16},{1,17},{2,18},{3,19},{4,20},{5,21},{6,22},{7,23},{8,24},{9,... | collective-permute-start | bytes 7323656 | tf_op jit(solution)/shard_map/cond/branch_4_fun/ppermute | solution.py:434

commit v4 on v3

--- a/solution.py
+++ b/solution.py
@@ -281,24 +281,35 @@
     )(me, number, count, req, home, maps, heat)
 
 
-def choose_kernel(table_ref, *refs):
-    *piles, out_ref = refs
+def choose_kernel(table_hbm, *refs):
+    piles, (out_ref, table, pile, sems) = refs[:4], refs[4:]
+    copies = [pltpu.make_async_copy(table_hbm, table, sems.at[4])]
+    copies += [pltpu.make_async_copy(p, pile.at[k], sems.at[k]) for k, p in enumerate(piles)]
+    for c in copies:
+        c.start()
+    for c in copies:
+        c.wait()
     lane = lax.broadcasted_iota(jnp.int32, (64, 32), 1)
-    pick = jnp.where(table_ref[:, 0:32] == lane, 1.0, 0.0).astype(bf16)
+    pick = jnp.where(table[:, 0:32] == lane, 1.0, 0.0).astype(bf16)
 
     @pl.loop(0, 9)
     def _(k):
-        pile = jnp.concatenate([p[:, block(k, 1024)] for p in piles], axis=0)
-        out_ref[:, block(k, 1024)] = dot(pick, pile).astype(bf16)
+        rows = jnp.concatenate([pile[p, :, block(k, 1024)] for p in range(4)], axis=0)
+        out_ref[:, block(k, 1024)] = dot(pick, rows).astype(bf16)
 
 
 def choose(table, *piles):
-    vm = pl.BlockSpec(memory_space=pltpu.VMEM)
+    hb = pl.BlockSpec(memory_space=pltpu.HBM)
     return pl.pallas_call(
         choose_kernel,
         out_shape=jax.ShapeDtypeStruct((64, 9216), bf16),
-        in_specs=[vm] * 5,
-        out_specs=vm,
+        in_specs=[hb] * 5,
+        out_specs=pl.BlockSpec(memory_space=pltpu.VMEM),
+        scratch_shapes=[
+            pltpu.VMEM((64, 128), jnp.int32),
+            pltpu.VMEM((4, 8, 9216), bf16),
+            pltpu.SemaphoreType.DMA((5,)),
+        ],
         compiler_params=pltpu.CompilerParams(vmem_limit_bytes=8 * 1024 * 1024),
         cost_estimate=pl.CostEstimate(flops=40000000, bytes_accessed=2000000, transcendentals=0),
     )(table, *piles)
@@ -382,10 +393,10 @@
     def load(k, lo, n):
         return pltpu.make_async_copy(t_hbm.at[pl.ds(lo, n)], theirs.at[pl.ds(lo, n)], asem.at[k])
 
-    def mixed(lo, n):
-        @pl.loop(0, n // 32)
+    def mixed(lo, n, m):
+        @pl.loop(0, n // m)
         def _(q):
-            r = pl.ds(pl.multiple_of(lo + q * 32, 32), 32)
+            r = pl.ds(pl.multiple_of(lo + q * m, 32), m)
             wide[r, :] = base_ref[r, :] + 0.5 * theirs[r, :].astype(f32)
 
     loads = [load(k, lo, n) for k, (lo, n) in enumerate(PIECES + ((ROW_STEM, 160),))]
@@ -394,11 +405,11 @@
     saves = []
     for k, (lo, n) in enumerate(PIECES):
         loads[k].wait()
-        mixed(lo, n)
+        mixed(lo, n, 128)
         saves.append(pltpu.make_async_copy(wide.at[pl.ds(lo, n)], new_hbm.at[pl.ds(lo, n)], osem.at[k]))
         saves[-1].start()
     loads[-1].wait()
-    mixed(ROW_STEM, 160)
+    mixed(ROW_STEM, 160, 160)
     last = len(PIECES)
     saves.append(pltpu.make_async_copy(wide.at[pl.ds(ROW_STEM, 128)], nstem_hbm, osem.at[last]))
     saves.append(pltpu.make_async_copy(wide.at[pl.ds(ROW_HEAD, 16)], nhead_hbm, osem.at[last + 1]))

time: 89.6 us -> 89.7 us (level)
  no operation moved by 1% of the time
where the time goes in v4:
time: 89.7 us; the launch traced here: 89.3 us
  Pallas kernels  38.8 us (43%)
  waiting for transfers between devices  29.3 us (33%)
  starting transfers between devices  18.7 us (21%)
  between operations  2.17 us (2%)
    all_to_all x2, waiting for transfers between devices, among(): lax.all_to_all(array, 'dev', split_axis=0, concat_axis=0, axis_index_grou...  27.1 us
    pallas_call x1, Pallas kernels, main_call(): pl.pallas_call(functools.partial(main_kernel, U=U, UB=UB, HU=HU, HV=HV, O...  25.4 us
    all_to_all x2, starting transfers between devices, among(): lax.all_to_all(array, 'dev', split_axis=0, concat_axis=0, axis_index_grou...  11.5 us
    ppermute x3, starting transfers between devices, gather(): lax.ppermute(mine, 'dev', [(i, i ^ m << shift) for i in range(32)])  4.32 us
    pallas_call x1, Pallas kernels, mix(): pl.pallas_call(mix_kernel, out_shape=(S((4608, 256), f32), S((128, 256),...  3.92 us
    pallas_call x1, Pallas kernels, choose(): pl.pallas_call(choose_kernel, out_shape=jax.ShapeDtypeStruct((64, 9216),...  3.77 us
    pallas_call x1, Pallas kernels, pack(): pl.pallas_call(pack_kernel, out_shape=jax.ShapeDtypeStruct((PACKED, 256),...  3.6 us
    ppermute x1, starting transfers between devices, swap(): return lax.ppermute(array, BOTH, [(i, i ^ 1 << bit) for i in range(256)])  2.93 us
  transfers between devices with their start and end apart: 6, of which 3 were waited for; matrix products, arithmetic and copies ran while one was open for 0% of the time, Pallas kernels for 33%

profile of v4, /device:TPU:1, one launch (start us, length us, event | category | flops | bytes accessed | tf_op | source)
XLA Modules:
  0.0 89.3 jit_solution(9097770507643678830)
XLA Ops:
  1.9 2.1 %shard_map.161 = (s32[8,8,128]{2,1,0:T(8,128)}, bf16[32,64]{1,0:T(8,128)(2,1)S(1)}, f32[32,128]{1,0:T(8,128)S(1)}, bf16[8,9216]{1,0:T(8,128)(2,1)S(1)}) custom-call(s32[1]{0:T(128)} %bitcast.28.me_ref, s32[1]{0:T(128)} %bitcast.38.step_ref, s32[1]{0:T(128)S(6)} %copy.77.count_ref, s32[1,32]{1,0:T(1,128)} %req_hbm.1, s32[1,256]{1,0:T(1,128)} %home_hbm.1, ...), custom_call_target="tpu_custom_call" | custom-call | tf_op jit(solution)/shard_map/pallas_call | solution.py:267
  4.0 16.7 %conditional.2 = (bf16[4768,256]{1,0:T(8,128)(2,1)}, s32[8,8,128]{2,1,0:T(8,128)}, bf16[8,9216]{1,0:T(8,128)(2,1)}, bf16[8,9216]{1,0:T(8,128)(2,1)}, bf16[8,9216]{1,0:T(8,128)(2,1)}) conditional(s32[]{:T(128)} %clamp.7, (f32[4608,256]{1,0:T(8,128)}, f32[128,256]{1,0:T(8,128)}, f32[16,256]{1,0:T(8,128)}, f32[3,1,256]{2,1,0:T(1,128)}, ...), branch_computations={%region_0.0_spmd, %region_1.0_spmd} | conditional | flops 1000000 | bytes 8867968 | solution.py:474
  4.0 3.6 %collective-permute-start.5 = (bf16[8,9216]{1,0:T(8,128)(2,1)S(1)}, bf16[8,9216]{1,0:T(8,128)(2,1)}, u32[]{:S(2)}, u32[]{:S(2)}) collective-permute-start(bf16[8,9216]{1,0:T(8,128)(2,1)S(1)} %get-tuple-element.227), channel_id=1, source_target_pairs={{0,24},{1,25},{2,26},{3,27},{4,28},{5,29},{6,30},{7,31},{8,16},{9,... | collective-permute-start | bytes 442376 | tf_op jit(solution)/shard_map/cond/branch_1_fun/ppermute | solution.py:454
  7.7 0.3 collective-permute-start.4
  8.0 0.3 collective-permute-start.3
  8.3 7.3 %all-to-all-start.1 = ((s32[8,8,128]{2,1,0:T(8,128)}), s32[8,8,128]{2,1,0:T(8,128)}, u32[]{:S(2)}, u32[]{:S(2)}) async-start(s32[8,8,128]{2,1,0:T(8,128)} %get-tuple-element.226), calls=%async_computation.1 | async-start | bytes 65536 | tf_op jit(solution)/shard_map/cond/branch_1_fun/all_to_all | solution.py:449
  15.6 3.6 %branch_1_fun.3 = bf16[4768,256]{1,0:T(8,128)(2,1)} custom-call(f32[4608,256]{1,0:T(8,128)} %get-tuple-element.222.conv_hbm, f32[128,256]{1,0:T(8,128)} %get-tuple-element.223.stem_hbm, f32[16,256]{1,0:T(8,128)} %get-tuple-element.224.head_hbm, f32[3,1,256]{2,1,0:T(1,128)} %get-tuple-element.225.bias_hbm), custom_call_target="tpu_custom_call" | custom-call | flops 1000000 | bytes 7000000 | tf_op jit(solution)/shard_map/cond/branch_1_fun/pallas_call | solution.py:372
  19.2 1.5 %all-to-all-done.1 = s32[8,8,128]{2,1,0:T(8,128)} async-done(((s32[8,8,128]{2,1,0:T(8,128)}), s32[8,8,128]{2,1,0:T(8,128)}, u32[]{:S(2)}, u32[]{:S(2)}) %all-to-all-start.1) | async-done | bytes 32800 | tf_op jit(solution)/shard_map/cond/branch_1_fun/all_to_all | solution.py:449
  20.7 0.0 collective-permute-done.5
  20.7 0.0 collective-permute-done.4
  20.7 0.0 collective-permute-done.3
  20.7 64.5 %conditional.3 = (bf16[4768,256]{1,0:T(8,128)(2,1)}, bf16[4608,256]{1,0:T(8,128)(2,1)}, f32[4768,256]{1,0:T(8,128)S(1)}, bf16[128,256]{1,0:T(8,128)(2,1)}, bf16[...) conditional(s32[]{:T(128)} %clamp.6, (bf16[4768,256]{1,0:T(8,128)(2,1)}, ...), branch_computations={%region_2.0_spmd, %region_3.0_spmd, %region_4.0_spmd, %region_5.0_... | conditional | flops 16039999488 | bytes 31906124 | solution.py:478
  20.9 0.0 copy-start.4
  20.9 0.0 copy-start.12
  21.0 0.0 copy-start.20
  21.0 3.8 %branch_4_fun.2 = bf16[64,9216]{1,0:T(8,128)(2,1)} custom-call(s32[64,128]{1,0:T(8,128)} %bitcast.12.table_hbm, bf16[8,9216]{1,0:T(8,128)(2,1)S(1)} %get-tuple-element.300.refs_0_, bf16[8,9216]{1,0:T(8,128)(2,1)} %get-tuple-element.301.refs_1_, bf16[8,9216]{1,0:T(8,128)(2,1)} %get-tuple-element.302.refs_2_, bf16[8,9216]{1,0:T(8,128)(2,1)} %get-tuple-element.303.refs_3_), custom_call_target="tpu_custom_call" | custom-call | flops 40000000 | bytes 2000000 | tf_op jit(solution)/shard_map/cond/branch_4_fun/pallas_call | solution.py:303
  24.7 4.3 %all-to-all-start.6 = ((bf16[8,8,9216]{2,1,0:T(8,128)(2,1)}), bf16[8,8,9216]{2,1,0:T(8,128)(2,1)S(1)}, u32[]{:S(2)}, u32[]{:S(2)}) async-start(bf16[8,8,9216]{2,1,0:T(8,128)(2,1)} %bitcast.13), calls=%async_computation.6 | async-start | bytes 2359296 | tf_op jit(solution)/shard_map/cond/branch_4_fun/all_to_all | solution.py:449
  29.0 2.9 %collective-permute-start.10 = (bf16[4768,256]{1,0:T(8,128)(2,1)}, bf16[4768,256]{1,0:T(8,128)(2,1)}, u32[]{:S(2)}, u32[]{:S(2)}) collective-permute-start(bf16[4768,256]{1,0:T(8,128)(2,1)} %get-tuple-element.296.w_hbm), channel_id=1, source_target_pairs={{0,16},{1,17},{2,18},{3,19},{4,20},{5,21},{6,22},{7,23},{8,24},{9,... | collective-permute-start | bytes 7323656 | tf_op jit(solution)/shard_map/cond/branch_4_fun/ppermute | solution.py:445
  31.9 25.6 %all-to-all-done.6 = bf16[8,8,9216]{2,1,0:T(8,128)(2,1)S(1)} async-done(((bf16[8,8,9216]{2,1,0:T(8,128)(2,1)}), bf16[8,8,9216]{2,1,0:T(8,128)(2,1)S(1)}, u32[]{:S(2)}, u32[]{:S(2)}) %all-to-all-start.6) | async-done | bytes 1179680 | tf_op jit(solution)/shard_map/cond/branch_4_fun/all_to_all | solution.py:449
  57.5 0.0 copy-done.4
  57.5 0.0 copy-done.12
  57.5 0.0 copy-done.20
  57.6 25.4 %branch_4_fun.3 = (bf16[4608,256]{1,0:T(8,128)(2,1)}, f32[4768,256]{1,0:T(8,128)S(1)}, bf16[128,256]{1,0:T(8,128)(2,1)}, bf16[16,256]{1,0:T(8,128)(2,1)}, bf16[3,256]{1,0:T(4,128)(2,1)}) custom-call(f32[32,128]{1,0:T(8,128)S(1)} %get-tuple-element.297.weight_ref, bf16[32,64]{1,0:T(8,128)(2,1)S(1)} %get-tuple-element.298.sel_ref, ...), custom_call_target="tpu_custom_call" | custom-call | flops 16000000000 | bytes 16000000 | tf_op jit(solution)/shard_map/cond/branch_4_fun/pallas_call | solution.py:193
  83.0 2.2 %collective-permute-done.10 = bf16[4768,256]{1,0:T(8,128)(2,1)} collective-permute-done((bf16[4768,256]{1,0:T(8,128)(2,1)}, bf16[4768,256]{1,0:T(8,128)(2,1)}, u32[]{:S(2)}, u32[]{:S(2)}) %collective-permute-start.10) | collective-permute-done | bytes 2441248 | tf_op jit(solution)/shard_map/cond/branch_4_fun/ppermute | solution.py:445
  85.2 3.9 %shard_map.162 = (f32[4608,256]{1,0:T(8,128)}, f32[128,256]{1,0:T(8,128)}, f32[16,256]{1,0:T(8,128)}, f32[3,1,256]{2,1,0:T(1,128)}) custom-call(bf16[4768,256]{1,0:T(8,128)(2,1)} %get-tuple-element.400.t_hbm, f32[4768,256]{1,0:T(8,128)S(1)} %get-tuple-element.401.base_ref), custom_call_target="tpu_custom_call" | custom-call | flops 1000000 | bytes 12000000 | tf_op jit(solution)/shard_map/pallas_call | solution.py:428
Async XLA Ops:
  4.0 16.6 %collective-permute-start.5 = (bf16[8,9216]{1,0:T(8,128)(2,1)S(1)}, bf16[8,9216]{1,0:T(8,128)(2,1)}, u32[]{:S(2)}, u32[]{:S(2)}) collective-permute-start(bf16[8,9216]{1,0:T(8,128)(2,1)S(1)} %get-tuple-element.227), channel_id=1, source_target_pairs={{0,24},{1,25},{2,26},{3,27},{4,28},{5,29},{6,30},{7,31},{8,16},{9,... | collective-permute-start | bytes 442376 | tf_op jit(solution)/shard_map/cond/branch_1_fun/ppermute | solution.py:454
  7.7 13.0 %collective-permute-start.4 = (bf16[8,9216]{1,0:T(8,128)(2,1)S(1)}, bf16[8,9216]{1,0:T(8,128)(2,1)}, u32[]{:S(2)}, u32[]{:S(2)}) collective-permute-start(bf16[8,9216]{1,0:T(8,128)(2,1)S(1)} %get-tuple-element.227), channel_id=1, source_target_pairs={{0,16},{1,17},{2,18},{3,19},{4,20},{5,21},{6,22},{7,23},{8,24},{9,... | collective-permute-start | bytes 442376 | tf_op jit(solution)/shard_map/cond/branch_1_fun/ppermute | solution.py:454
  8.0 12.7 %collective-permute-start.3 = (bf16[8,9216]{1,0:T(8,128)(2,1)S(1)}, bf16[8,9216]{1,0:T(8,128)(2,1)}, u32[]{:S(2)}, u32[]{:S(2)}) collective-permute-start(bf16[8,9216]{1,0:T(8,128)(2,1)S(1)} %get-tuple-element.227), channel_id=1, source_target_pairs={{0,8},{1,9},{2,10},{3,11},{4,12},{5,13},{6,14},{7,15},{8,0},{9,1},... | collective-permute-start | bytes 442376 | tf_op jit(solution)/shard_map/cond/branch_1_fun/ppermute | solution.py:454
  8.3 12.3 %all-to-all-start.1 = ((s32[8,8,128]{2,1,0:T(8,128)}), s32[8,8,128]{2,1,0:T(8,128)}, u32[]{:S(2)}, u32[]{:S(2)}) async-start(s32[8,8,128]{2,1,0:T(8,128)} %get-tuple-element.226), calls=%async_computation.1 | async-start | bytes 65536 | tf_op jit(solution)/shard_map/cond/branch_1_fun/all_to_all | solution.py:449
  20.9 36.6 %copy-start.4 = (f32[128,256]{1,0:T(8,128)S(1)}, f32[128,256]{1,0:T(8,128)}, u32[]{:S(2)}) copy-start(f32[128,256]{1,0:T(8,128)} %get-tuple-element.306.stem_ref) | copy-start | bytes 393220 | tf_op jit(solution)/shard_map/cond
  20.9 36.6 %copy-start.12 = (f32[16,256]{1,0:T(8,128)S(1)}, f32[16,256]{1,0:T(8,128)}, u32[]{:S(2)}) copy-start(f32[16,256]{1,0:T(8,128)} %get-tuple-element.307.head_ref) | copy-start | bytes 49156 | tf_op jit(solution)/shard_map/cond
  21.0 36.6 %copy-start.20 = (f32[3,1,256]{2,1,0:T(1,128)S(1)}, f32[3,1,256]{2,1,0:T(1,128)}, u32[]{:S(2)}) copy-start(f32[3,1,256]{2,1,0:T(1,128)} %get-tuple-element.304.bias_ref) | copy-start | bytes 9220 | tf_op jit(solution)/shard_map/cond
  24.7 32.8 %all-to-all-start.6 = ((bf16[8,8,9216]{2,1,0:T(8,128)(2,1)}), bf16[8,8,9216]{2,1,0:T(8,128)(2,1)S(1)}, u32[]{:S(2)}, u32[]{:S(2)}) async-start(bf16[8,8,9216]{2,1,0:T(8,128)(2,1)} %bitcast.13), calls=%async_computation.6 | async-start | bytes 2359296 | tf_op jit(solution)/shard_map/cond/branch_4_fun/all_to_all | solution.py:449
  29.0 56.2 %collective-permute-start.10 = (bf16[4768,256]{1,0:T(8,128)(2,1)}, bf16[4768,256]{1,0:T(8,128)(2,1)}, u32[]{:S(2)}, u32[]{:S(2)}) collective-permute-start(bf16[4768,256]{1,0:T(8,128)(2,1)} %get-tuple-element.296.w_hbm), channel_id=1, source_target_pairs={{0,16},{1,17},{2,18},{3,19},{4,20},{5,21},{6,22},{7,23},{8,24},{9,... | collective-permute-start | bytes 7323656 | tf_op jit(solution)/shard_map/cond/branch_4_fun/ppermute | solution.py:445

commit v5 on v4

--- a/solution.py
+++ b/solution.py
@@ -185,7 +185,7 @@
             c.wait()
 
 
-def main_call(weight, sel, got, packed, bias, conv, stem, head, U=2, UB=2, HU=8, HV=4, ONE=False):
+def main_call(weight, sel, got, packed, bias, conv, stem, head, U=2, UB=2, HU=8, HV=2, ONE=False):
     vm = pl.BlockSpec(memory_space=pltpu.VMEM)
     hb = pl.BlockSpec(memory_space=pltpu.HBM)
     S = jax.ShapeDtypeStruct
@@ -213,31 +213,51 @@
 Y_BITS = (3, 4)
 
 
-def prep_kernel(me_ref, step_ref, count_ref, req_hbm, home_hbm, maps_hbm, heat_hbm, asked_ref, sel_ref, weight_ref, mine_ref,
-                req, home, heat, maps, wide, sems):
-    copies = [
-        pltpu.make_async_copy(src, dst, sems.at[k])
-        for k, (src, dst) in enumerate((
-            (maps_hbm, maps), (heat_hbm, heat), (req_hbm, req), (home_hbm, home),
-        ))
-    ]
+def spread_kernel(maps_hbm, heat_hbm, mine_ref, heat, maps, wide, sems):
+    copies = [pltpu.make_async_copy(maps_hbm, maps, sems.at[0]), pltpu.make_async_copy(heat_hbm, heat, sems.at[1])]
     for c in copies:
         c.start()
-    for c in copies[2:]:
+    copies[0].wait()
+    wide[...] = maps[...].reshape(512, 128).astype(f32)
+    for p in range(64):
+        mine_ref[:, p * 128:(p + 1) * 128] = wide[pl.ds(p, 8, stride=64), :].astype(bf16)
+    copies[1].wait()
+    mine_ref[:, 8192:9216] = heat[...]
+
+
+def spread(maps, heat):
+    vm = pl.BlockSpec(memory_space=pltpu.VMEM)
+    hb = pl.BlockSpec(memory_space=pltpu.HBM)
+    return pl.pallas_call(
+        spread_kernel,
+        out_shape=jax.ShapeDtypeStruct((8, 9216), bf16),
+        in_specs=[hb, hb],
+        out_specs=vm,
+        scratch_shapes=[
+            pltpu.VMEM((8, 1024), bf16),
+            pltpu.VMEM((8, 64, 128), bf16),
+            pltpu.VMEM((512, 128), f32),
+            pltpu.SemaphoreType.DMA((2,)),
+        ],
+        compiler_params=pltpu.CompilerParams(vmem_limit_bytes=60 * 1024 * 1024),
+    )(maps, heat)
+
+
+def route_kernel(along, me_ref, count_ref, req_hbm, home_hbm, asked_ref, sel_ref, weight_ref, req, home, sems):
+    copies = [pltpu.make_async_copy(req_hbm, req, sems.at[0]), pltpu.make_async_copy(home_hbm, home, sems.at[1])]
+    for c in copies:
+        c.start()
+    for c in copies:
         c.wait()
     count = count_ref[0]
-    bit = step_ref[0] & 7
-    on_y = ((bit == Y_BITS[0]) | (bit == Y_BITS[1])).astype(jnp.int32)
     i = lax.broadcasted_iota(jnp.int32, (32, 32), 0)
     j = lax.broadcasted_iota(jnp.int32, (32, 32), 1)
     wanted = jnp.sum(jnp.where(i == j, req[...], 0), axis=1, keepdims=True)
     lane = lax.broadcasted_iota(jnp.int32, (32, 256), 1)
     pos = jnp.sum(jnp.where(lane == wanted, home[...], 0), axis=1, keepdims=True)
     owner = pos >> 3
-    along = 1 + 2 * on_y
-    other = 4 - along
     here = (me_ref[0] >> along) & 3
-    column = ((owner >> other) & 3) * 2 + (owner & 1)
+    column = ((owner >> (4 - along)) & 3) * 2 + (owner & 1)
     row = (((owner >> along) & 3) ^ here) * 8 + (pos & 7)
     across_lanes = jnp.sum(jnp.where(i == j, column, 0), axis=0, keepdims=True)
     live = lax.broadcasted_iota(jnp.int32, (32, 1), 0) < count
@@ -251,34 +271,22 @@
     value = jnp.broadcast_to((row + 1).astype(f32), (32, 128)).astype(bf16)
     asked = lax.dot_general(pick.astype(bf16), value, TN, preferred_element_type=f32)
     asked_ref[...] = (asked.astype(jnp.int32) - 1).reshape(8, 8, 128)
-    copies[0].wait()
-    wide[...] = maps[...].reshape(512, 128).astype(f32)
-    for p in range(64):
-        mine_ref[:, p * 128:(p + 1) * 128] = wide[pl.ds(p, 8, stride=64), :].astype(bf16)
-    copies[1].wait()
-    mine_ref[:, 8192:9216] = heat[...]
-
-
-def prep(me, number, count, req, home, maps, heat):
+
+
+def route(along, me, count, req, home):
     vm = pl.BlockSpec(memory_space=pltpu.VMEM)
     sm = pl.BlockSpec(memory_space=pltpu.SMEM)
     hb = pl.BlockSpec(memory_space=pltpu.HBM)
     S = jax.ShapeDtypeStruct
     return pl.pallas_call(
-        prep_kernel,
-        out_shape=(S((8, 8, 128), jnp.int32), S((32, 64), bf16), S((32, 128), f32), S((8, 9216), bf16)),
-        in_specs=[sm, sm, sm, hb, hb, hb, hb],
-        out_specs=(vm, vm, vm, vm),
-        scratch_shapes=[
-            pltpu.VMEM((1, 32), jnp.int32),
-            pltpu.VMEM((1, 256), jnp.int32),
-            pltpu.VMEM((8, 1024), bf16),
-            pltpu.VMEM((8, 64, 128), bf16),
-            pltpu.VMEM((512, 128), f32),
-            pltpu.SemaphoreType.DMA((4,)),
-        ],
-        compiler_params=pltpu.CompilerParams(vmem_limit_bytes=60 * 1024 * 1024),
-    )(me, number, count, req, home, maps, heat)
+        functools.partial(route_kernel, along),
+        out_shape=(S((8, 8, 128), jnp.int32), S((32, 64), bf16), S((32, 128), f32)),
+        in_specs=[sm, sm, hb, hb],
+        out_specs=(vm, vm, vm),
+        scratch_shapes=[pltpu.VMEM((1, 32), jnp.int32), pltpu.VMEM((1, 256), jnp.int32), pltpu.SemaphoreType.DMA((2,))],
+        compiler_params=pltpu.CompilerParams(vmem_limit_bytes=8 * 1024 * 1024),
+        cost_estimate=pl.CostEstimate(flops=1000000, bytes_accessed=100000, transcendentals=0),
+    )(me, count, req, home)
 
 
 def choose_kernel(table_hbm, *refs):
@@ -449,12 +457,13 @@
     return lax.all_to_all(array, "dev", split_axis=0, concat_axis=0, axis_index_groups=groups, tiled=True)
 
 
-def gather(on_y, asked, mine, conv, stem, head, bias):
+def gather(on_y, me, counts, requests, home, mine, conv, stem, head, bias):
     shift, groups = (3, SAME_Y) if on_y else (1, SAME_Z)
     others = [lax.ppermute(mine, "dev", [(i, i ^ (m << shift)) for i in range(32)]) for m in (1, 2, 3)]
+    asked, sel, weight = route(shift, me, counts, requests, home)
     table = among(asked, groups)
     packed = pack(conv, stem, head, bias)
-    return packed, table, *others
+    return packed, sel, weight, table, *others
 
 
 def step(bit, weight, sel, table, mine, one, two, three, packed, bias, conv, stem, head):
@@ -470,10 +479,10 @@
     bit = step_number & 7
     on_y = ((bit == Y_BITS[0]) | (bit == Y_BITS[1])).astype(jnp.int32)
     me = lax.axis_index("dev").astype(jnp.int32)
-    asked, sel, weight, mine = prep(me.reshape(1), step_number.reshape(1), counts, requests, home, maps, heat)
-    packed, table, *others = lax.switch(
+    mine = spread(maps, heat)
+    packed, sel, weight, table, *others = lax.switch(
         on_y, [functools.partial(gather, 0), functools.partial(gather, 1)],
-        asked, mine, conv, stem, head, bias,
+        me.reshape(1), counts, requests, home, mine, conv, stem, head, bias,
     )
     outs = lax.switch(
         bit, [functools.partial(step, b) for b in range(8)],

time: 89.7 us -> 90.5 us (level)
  Pallas kernels: 38.8 us -> 40.5 us
    pallas_call x1 -> x2, Pallas kernels: 2.06 us -> 3.52 us  [the longest x1 2.43 us: route(): pl.pallas_call(functools.partial(route_kernel, along), out_shape=(S((8, 8...]
  transfers between devices with their start and end apart: 6 -> 6, of which waited for: 3 -> 3; matrix products, arithmetic and copies ran while one was open for 0% -> 0% of each run, Pallas kernels for 33% -> 35%
where the time goes in v5:
time: 90.5 us; the launch traced here: 90.2 us
  Pallas kernels  40.5 us (45%)
  waiting for transfers between devices  29 us (32%)
  starting transfers between devices  18.8 us (21%)
  between operations  1.53 us (2%)
    all_to_all x2, waiting for transfers between devices, among(): lax.all_to_all(array, 'dev', split_axis=0, concat_axis=0, axis_index_grou...  27.1 us
    pallas_call x1, Pallas kernels, main_call(): pl.pallas_call(functools.partial(main_kernel, U=U, UB=UB, HU=HU, HV=HV, O...  25.7 us
    all_to_all x2, starting transfers between devices, among(): lax.all_to_all(array, 'dev', split_axis=0, concat_axis=0, axis_index_grou...  11.5 us
    ppermute x3, starting transfers between devices, gather(): lax.ppermute(mine, 'dev', [(i, i ^ m << shift) for i in range(32)])  4.32 us
    pallas_call x1, Pallas kernels, mix(): pl.pallas_call(mix_kernel, out_shape=(S((4608, 256), f32), S((128, 256),...  3.92 us
    pallas_call x1, Pallas kernels, choose(): pl.pallas_call(choose_kernel, out_shape=jax.ShapeDtypeStruct((64, 9216),...  3.77 us
    pallas_call x1, Pallas kernels, pack(): pl.pallas_call(pack_kernel, out_shape=jax.ShapeDtypeStruct((PACKED, 256),...  3.6 us
    ppermute x1, starting transfers between devices, swap(): return lax.ppermute(array, BOTH, [(i, i ^ 1 << bit) for i in range(256)])  2.93 us
  transfers between devices with their start and end apart: 6, of which 3 were waited for; matrix products, arithmetic and copies ran while one was open for 0% of the time, Pallas kernels for 35%

profile of v5, /device:TPU:1, one launch (start us, length us, event | category | flops | bytes accessed | tf_op | source)
XLA Modules:
  0.0 90.2 jit_solution(4557332159872168652)
XLA Ops:
  1.3 1.1 %shard_map.161 = bf16[8,9216]{1,0:T(8,128)(2,1)S(1)} custom-call(bf16[8,64,128]{2,1,0:T(8,128)(2,1)} %maps_hbm.1, bf16[8,1024]{1,0:T(8,128)(2,1)} %heat_hbm.1), custom_call_target="tpu_custom_call" | custom-call | tf_op jit(solution)/shard_map/pallas_call | solution.py:231
  2.4 19.1 %conditional.2 = (bf16[4768,256]{1,0:T(8,128)(2,1)}, bf16[32,64]{1,0:T(8,128)(2,1)S(1)}, f32[32,128]{1,0:T(8,128)S(1)}, s32[8,8,128]{2,1,0:T(8,128)}, bf16[8,921...) conditional(s32[]{:T(128)} %clamp.7, (f32[4608,256]{1,0:T(8,128)}, f32[128,256]{1,0:T(8,128)}, ...), branch_computations={%region_0.0_spmd, %region_1.0_spmd} | conditional | flops 2000000 | bytes 8967984 | solution.py:483
  2.4 3.6 %collective-permute-start.5 = (bf16[8,9216]{1,0:T(8,128)(2,1)S(1)}, bf16[8,9216]{1,0:T(8,128)(2,1)}, u32[]{:S(2)}, u32[]{:S(2)}) collective-permute-start(bf16[8,9216]{1,0:T(8,128)(2,1)S(1)} %get-tuple-element.251), channel_id=1, source_target_pairs={{0,24},{1,25},{2,26},{3,27},{4,28},{5,29},{6,30},{7,31},{8,16},{9,... | collective-permute-start | bytes 442376 | tf_op jit(solution)/shard_map/cond/branch_1_fun/ppermute | solution.py:462
  6.1 0.3 collective-permute-start.4
  6.4 0.3 collective-permute-start.3
  6.7 2.4 %branch_1_fun.5 = (s32[8,8,128]{2,1,0:T(8,128)}, bf16[32,64]{1,0:T(8,128)(2,1)S(1)}, f32[32,128]{1,0:T(8,128)S(1)}) custom-call(s32[1]{0:T(128)} %get-tuple-element.244.me_ref, s32[1]{0:T(128)} %get-tuple-element.245.count_ref, s32[1,32]{1,0:T(1,128)} %get-tuple-element.246.req_hbm, s32[1,256]{1,0:T(1,128)} %get-tuple-element.247.home_hbm), custom_call_target="tpu_custom_call" | custom-call | flops 1000000 | bytes 100000 | tf_op jit(solution)/shard_map/cond/branch_1_fun/pallas_call | solution.py:281
  9.2 7.3 %all-to-all-start.1 = ((s32[8,8,128]{2,1,0:T(8,128)}), s32[8,8,128]{2,1,0:T(8,128)}, u32[]{:S(2)}, u32[]{:S(2)}) async-start(s32[8,8,128]{2,1,0:T(8,128)} %get-tuple-element.250), calls=%async_computation.1 | async-start | bytes 65536 | tf_op jit(solution)/shard_map/cond/branch_1_fun/all_to_all | solution.py:457
  16.4 3.6 %branch_1_fun.4 = bf16[4768,256]{1,0:T(8,128)(2,1)} custom-call(f32[4608,256]{1,0:T(8,128)} %get-tuple-element.240.conv_hbm, f32[128,256]{1,0:T(8,128)} %get-tuple-element.241.stem_hbm, f32[16,256]{1,0:T(8,128)} %get-tuple-element.242.head_hbm, f32[3,1,256]{2,1,0:T(1,128)} %get-tuple-element.243.bias_hbm), custom_call_target="tpu_custom_call" | custom-call | flops 1000000 | bytes 7000000 | tf_op jit(solution)/shard_map/cond/branch_1_fun/pallas_call | solution.py:380
  20.1 1.5 %all-to-all-done.1 = s32[8,8,128]{2,1,0:T(8,128)} async-done(((s32[8,8,128]{2,1,0:T(8,128)}), s32[8,8,128]{2,1,0:T(8,128)}, u32[]{:S(2)}, u32[]{:S(2)}) %all-to-all-start.1) | async-done | bytes 32800 | tf_op jit(solution)/shard_map/cond/branch_1_fun/all_to_all | solution.py:457
  21.5 0.0 collective-permute-done.5
  21.5 0.0 collective-permute-done.4
  21.5 0.0 collective-permute-done.3
  21.5 64.5 %conditional.3 = (bf16[4768,256]{1,0:T(8,128)(2,1)}, bf16[4608,256]{1,0:T(8,128)(2,1)}, f32[4768,256]{1,0:T(8,128)S(1)}, bf16[128,256]{1,0:T(8,128)(2,1)}, bf16[...) conditional(s32[]{:T(128)} %clamp.6, (bf16[4768,256]{1,0:T(8,128)(2,1)}, ...), branch_computations={%region_2.0_spmd, %region_3.0_spmd, %region_4.0_spmd, %region_5.0_... | conditional | flops 16039999488 | bytes 31906124 | solution.py:487
  21.8 0.0 copy-start.4
  21.8 0.0 copy-start.12
  21.8 0.0 copy-start.20
  21.8 3.8 %branch_4_fun.2 = bf16[64,9216]{1,0:T(8,128)(2,1)} custom-call(s32[64,128]{1,0:T(8,128)} %bitcast.12.table_hbm, bf16[8,9216]{1,0:T(8,128)(2,1)S(1)} %get-tuple-element.324.refs_0_, bf16[8,9216]{1,0:T(8,128)(2,1)} %get-tuple-element.325.refs_1_, bf16[8,9216]{1,0:T(8,128)(2,1)} %get-tuple-element.326.refs_2_, bf16[8,9216]{1,0:T(8,128)(2,1)} %get-tuple-element.327.refs_3_), custom_call_target="tpu_custom_call" | custom-call | flops 40000000 | bytes 2000000 | tf_op jit(solution)/shard_map/cond/branch_4_fun/pallas_call | solution.py:311
  25.6 4.3 %all-to-all-start.6 = ((bf16[8,8,9216]{2,1,0:T(8,128)(2,1)}), bf16[8,8,9216]{2,1,0:T(8,128)(2,1)S(1)}, u32[]{:S(2)}, u32[]{:S(2)}) async-start(bf16[8,8,9216]{2,1,0:T(8,128)(2,1)} %bitcast.13), calls=%async_computation.6 | async-start | bytes 2359296 | tf_op jit(solution)/shard_map/cond/branch_4_fun/all_to_all | solution.py:457
  29.8 2.9 %collective-permute-start.10 = (bf16[4768,256]{1,0:T(8,128)(2,1)}, bf16[4768,256]{1,0:T(8,128)(2,1)}, u32[]{:S(2)}, u32[]{:S(2)}) collective-permute-start(bf16[4768,256]{1,0:T(8,128)(2,1)} %get-tuple-element.320.w_hbm), channel_id=1, source_target_pairs={{0,16},{1,17},{2,18},{3,19},{4,20},{5,21},{6,22},{7,23},{8,24},{9,... | collective-permute-start | bytes 7323656 | tf_op jit(solution)/shard_map/cond/branch_4_fun/ppermute | solution.py:453
  32.8 25.6 %all-to-all-done.6 = bf16[8,8,9216]{2,1,0:T(8,128)(2,1)S(1)} async-done(((bf16[8,8,9216]{2,1,0:T(8,128)(2,1)}), bf16[8,8,9216]{2,1,0:T(8,128)(2,1)S(1)}, u32[]{:S(2)}, u32[]{:S(2)}) %all-to-all-start.6) | async-done | bytes 1179680 | tf_op jit(solution)/shard_map/cond/branch_4_fun/all_to_all | solution.py:457
  58.4 0.0 copy-done.4
  58.4 0.0 copy-done.12
  58.4 0.0 copy-done.20
  58.4 25.7 %branch_4_fun.3 = (bf16[4608,256]{1,0:T(8,128)(2,1)}, f32[4768,256]{1,0:T(8,128)S(1)}, bf16[128,256]{1,0:T(8,128)(2,1)}, bf16[16,256]{1,0:T(8,128)(2,1)}, bf16[3,256]{1,0:T(4,128)(2,1)}) custom-call(f32[32,128]{1,0:T(8,128)S(1)} %get-tuple-element.321.weight_ref, bf16[32,64]{1,0:T(8,128)(2,1)S(1)} %get-tuple-element.322.sel_ref, ...), custom_call_target="tpu_custom_call" | custom-call | flops 16000000000 | bytes 16000000 | tf_op jit(solution)/shard_map/cond/branch_4_fun/pallas_call | solution.py:193
  84.1 2.0 %collective-permute-done.10 = bf16[4768,256]{1,0:T(8,128)(2,1)} collective-permute-done((bf16[4768,256]{1,0:T(8,128)(2,1)}, bf16[4768,256]{1,0:T(8,128)(2,1)}, u32[]{:S(2)}, u32[]{:S(2)}) %collective-permute-start.10) | collective-permute-done | bytes 2441248 | tf_op jit(solution)/shard_map/cond/branch_4_fun/ppermute | solution.py:453
  86.0 3.9 %shard_map.162 = (f32[4608,256]{1,0:T(8,128)}, f32[128,256]{1,0:T(8,128)}, f32[16,256]{1,0:T(8,128)}, f32[3,1,256]{2,1,0:T(1,128)}) custom-call(bf16[4768,256]{1,0:T(8,128)(2,1)} %get-tuple-element.420.t_hbm, f32[4768,256]{1,0:T(8,128)S(1)} %get-tuple-element.421.base_ref), custom_call_target="tpu_custom_call" | custom-call | flops 1000000 | bytes 12000000 | tf_op jit(solution)/shard_map/pallas_call | solution.py:436
Async XLA Ops:
  2.4 19.1 %collective-permute-start.5 = (bf16[8,9216]{1,0:T(8,128)(2,1)S(1)}, bf16[8,9216]{1,0:T(8,128)(2,1)}, u32[]{:S(2)}, u32[]{:S(2)}) collective-permute-start(bf16[8,9216]{1,0:T(8,128)(2,1)S(1)} %get-tuple-element.251), channel_id=1, source_target_pairs={{0,24},{1,25},{2,26},{3,27},{4,28},{5,29},{6,30},{7,31},{8,16},{9,... | collective-permute-start | bytes 442376 | tf_op jit(solution)/shard_map/cond/branch_1_fun/ppermute | solution.py:462
  6.1 15.5 %collective-permute-start.4 = (bf16[8,9216]{1,0:T(8,128)(2,1)S(1)}, bf16[8,9216]{1,0:T(8,128)(2,1)}, u32[]{:S(2)}, u32[]{:S(2)}) collective-permute-start(bf16[8,9216]{1,0:T(8,128)(2,1)S(1)} %get-tuple-element.251), channel_id=1, source_target_pairs={{0,16},{1,17},{2,18},{3,19},{4,20},{5,21},{6,22},{7,23},{8,24},{9,... | collective-permute-start | bytes 442376 | tf_op jit(solution)/shard_map/cond/branch_1_fun/ppermute | solution.py:462
  6.4 15.1 %collective-permute-start.3 = (bf16[8,9216]{1,0:T(8,128)(2,1)S(1)}, bf16[8,9216]{1,0:T(8,128)(2,1)}, u32[]{:S(2)}, u32[]{:S(2)}) collective-permute-start(bf16[8,9216]{1,0:T(8,128)(2,1)S(1)} %get-tuple-element.251), channel_id=1, source_target_pairs={{0,8},{1,9},{2,10},{3,11},{4,12},{5,13},{6,14},{7,15},{8,0},{9,1},... | collective-permute-start | bytes 442376 | tf_op jit(solution)/shard_map/cond/branch_1_fun/ppermute | solution.py:462
  9.2 12.3 %all-to-all-start.1 = ((s32[8,8,128]{2,1,0:T(8,128)}), s32[8,8,128]{2,1,0:T(8,128)}, u32[]{:S(2)}, u32[]{:S(2)}) async-start(s32[8,8,128]{2,1,0:T(8,128)} %get-tuple-element.250), calls=%async_computation.1 | async-start | bytes 65536 | tf_op jit(solution)/shard_map/cond/branch_1_fun/all_to_all | solution.py:457
  21.8 36.6 %copy-start.4 = (f32[128,256]{1,0:T(8,128)S(1)}, f32[128,256]{1,0:T(8,128)}, u32[]{:S(2)}) copy-start(f32[128,256]{1,0:T(8,128)} %get-tuple-element.330.stem_ref) | copy-start | bytes 393220 | tf_op jit(solution)/shard_map/cond
  21.8 36.6 %copy-start.12 = (f32[16,256]{1,0:T(8,128)S(1)}, f32[16,256]{1,0:T(8,128)}, u32[]{:S(2)}) copy-start(f32[16,256]{1,0:T(8,128)} %get-tuple-element.331.head_ref) | copy-start | bytes 49156 | tf_op jit(solution)/shard_map/cond
  21.8 36.6 %copy-start.20 = (f32[3,1,256]{2,1,0:T(1,128)S(1)}, f32[3,1,256]{2,1,0:T(1,128)}, u32[]{:S(2)}) copy-start(f32[3,1,256]{2,1,0:T(1,128)} %get-tuple-element.328.bias_ref) | copy-start | bytes 9220 | tf_op jit(solution)/shard_map/cond
  25.6 32.8 %all-to-all-start.6 = ((bf16[8,8,9216]{2,1,0:T(8,128)(2,1)}), bf16[8,8,9216]{2,1,0:T(8,128)(2,1)S(1)}, u32[]{:S(2)}, u32[]{:S(2)}) async-start(bf16[8,8,9216]{2,1,0:T(8,128)(2,1)} %bitcast.13), calls=%async_computation.6 | async-start | bytes 2359296 | tf_op jit(solution)/shard_map/cond/branch_4_fun/all_to_all | solution.py:457
  29.8 56.2 %collective-permute-start.10 = (bf16[4768,256]{1,0:T(8,128)(2,1)}, bf16[4768,256]{1,0:T(8,128)(2,1)}, u32[]{:S(2)}, u32[]{:S(2)}) collective-permute-start(bf16[4768,256]{1,0:T(8,128)(2,1)} %get-tuple-element.320.w_hbm), channel_id=1, source_target_pairs={{0,16},{1,17},{2,18},{3,19},{4,20},{5,21},{6,22},{7,23},{8,24},{9,... | collective-permute-start | bytes 7323656 | tf_op jit(solution)/shard_map/cond/branch_4_fun/ppermute | solution.py:453
